TPU v7x, 32 devices: a whole 2x2x4 slice. The times are simulated.
32 devices in a mesh: groups: 2 (over x), dp: 8 (over z, y), tensor: 2 (over core).
Axes of the slice: x: 2, y: 2, z: 4, core: 2. Of those that a mesh axis runs over, the one named last changes fastest.
Arguments:
- queries: bfloat16 [4096, 4096], P(('groups', 'dp'), 'tensor'), parts along dimension 0, may hold values from -6.5 to 6.5
- fresh_keys: bfloat16 [4096, 512], P(('groups', 'dp'), 'tensor'), parts along dimension 0, may hold values from -4 to 4
- fresh_values: bfloat16 [4096, 512], P(('groups', 'dp'), 'tensor'), parts along dimension 0, may hold values from -4 to 4
- key_pool_pages: bfloat16 [160, 128, 512], P(('groups', 'dp'), None, 'tensor'), parts along dimension 0, may hold values from -4 to 4
- value_pool_pages: bfloat16 [160, 128, 512], P(('groups', 'dp'), None, 'tensor'), parts along dimension 0, may hold values from -4 to 4
- block_table: int32 [16, 8], P(('groups', 'dp')), parts along dimension 0, may hold values from 0 to 9, as said below
- prefix_lengths: int32 [16], P('groups'), parts along dimension 0, may hold values from 0 to 1024, as said below
- out_weight: bfloat16 [4096, 4096], P('tensor', 'dp'), may hold values from -0.09375 to 0.09375
Outputs:
- output: bfloat16 [4096, 4096], P(('groups', 'dp'), 'tensor'), parts along dimension 0
There are 2 independent parts, one for each index of `groups`. A program takes and returns all parts, laid end to end along the dimension named above; an argument that names none is the same for every part. Nothing has to cross between parts.
Inputs may be any that keep to these rules, and one draw needn't show every extreme that they name: `block_table`: each row holds distinct pages of the request's own pool of 10 pages. `prefix_lengths`: some request has exactly 1024 cached tokens and some has none.
All inputs are finite; a program needn't handle non-finite values.
Results may differ from a plain program's by a relative error of at most 0.0095.
Values may be sent and summed in bfloat16 or wider, within the bound.
A program may use at most 128 MiB of HBM per device.

v0:
```python
import functools

import jax
import jax.numpy as jnp
from jax import lax
from jax.experimental import pallas as pl
from jax.experimental.pallas import tpu as pltpu
from jax.sharding import PartitionSpec as P

HEAD_SIZE = 128
QUERY_GROUP = 8
PAGE_TOKENS = 128
CHUNK = 256
SCALE = HEAD_SIZE ** (-0.5) * 1.4426950408889634
MASKED = -1e30


def kernel(
    line, q_ref, fk_ref, fv_ref, kp_ref, vp_ref, table_ref, len_ref, w_ref, out_ref,
    wbuf, act, stage, keys, values, bias,
    w_recv, w_next, w_side, own_send, act_recv, act_send, act_fwd, out_send, out_recv,
):
    group, dp, core = lax.axis_index("groups"), lax.axis_index("dp"), lax.axis_index("tensor")
    z, y = dp // 2, dp % 2
    half = group % 2
    cousin = group + 1 - 2 * half
    other = 1 - core
    peer = z * 2 + 1 - y
    shards = line // 2
    part, cols = w_ref.shape
    tokens = q_ref.shape[0]
    per_core = part // CHUNK
    per_half = per_core // 2
    own_core = z // shards
    own_slot = z - own_core * shards
    wide = act.shape[2] // 2
    step_cols = wide // per_core
    heads_per_step = step_cols // HEAD_SIZE
    heads_per_kv = QUERY_GROUP
    tile = min(cols, 256)
    tiles = cols // tile

    def remote(src, dst, send, recv, where):
        return pltpu.make_async_remote_copy(
            src_ref=src, dst_ref=dst, send_sem=send, recv_sem=recv,
            device_id=where, device_id_type=pl.DeviceIdType.MESH,
        )

    def rows(k):
        return pl.ds(pl.multiple_of(k * CHUNK, CHUNK), CHUNK)

    barrier = pltpu.get_barrier_semaphore()

    def greet(where):
        pl.semaphore_signal(barrier, inc=1, device_id=where, device_id_type=pl.DeviceIdType.MESH)

    greet((group, dp, other))
    greet((cousin, dp, core))
    greet((group, peer, core))

    @pl.when(z > 0)
    def _():
        greet((group, dp - 2, core))
        greet((group, dp - 2, other))

    @pl.when(z < line - 1)
    def _():
        greet((group, dp + 2, core))
        greet((group, dp + 2, other))

    neighbours = jnp.where(z > 0, 2, 0) + jnp.where(z < line - 1, 2, 0)
    pl.semaphore_wait(barrier, 3 + neighbours)

    def own_copy(k, side):
        slab = core * per_core + k
        where = (group, dp + 2 * side, own_core) if side else (group, dp, other)
        return remote(
            w_ref.at[rows(k)], wbuf.at[own_slot, rows(slab)],
            own_send.at[side + 1, k], w_recv.at[own_slot, slab], where,
        )

    def own_local(k):
        slab = core * per_core + k
        return pltpu.make_async_copy(
            w_ref.at[rows(k)], wbuf.at[own_slot, rows(slab)], w_recv.at[own_slot, slab]
        )

    def each_own(act_on):
        def one(j, carry):
            k = half * per_half + j

            @pl.when(z > 0)
            def _():
                act_on(own_copy(k, -1))

            @pl.when(z < line - 1)
            def _():
                act_on(own_copy(k, 1))

            return carry

        lax.fori_loop(0, per_half, one, 0)

        @pl.when(core != own_core)
        def _():
            lax.fori_loop(0, per_core, lambda k, carry: (act_on(own_copy(k, 0)), carry)[1], 0)

    each_own(lambda copy: copy.start())

    @pl.when(core == own_core)
    def _():
        lax.fori_loop(0, per_core, lambda k, carry: (own_local(k).start(), carry)[1], 0)

    def slab_of(i, which):
        return (i % 2) * per_core + which * per_half + i // 2

    def landed(slot, slab):
        remote(
            wbuf.at[slot, rows(slab)], wbuf.at[slot, rows(slab)],
            w_next.at[slot, slab], w_recv.at[slot, slab], (group, dp, other),
        ).wait_recv()

    def next_copy(slot, slab, step):
        return remote(
            wbuf.at[slot, rows(slab)], wbuf.at[slot, rows(slab)],
            w_next.at[slot, slab], w_recv.at[slot, slab], (group, dp + 2 * step, core),
        )

    def side_copy(slot, slab):
        return remote(
            wbuf.at[slot, rows(slab)], wbuf.at[slot, rows(slab)],
            w_side.at[slot, slab], w_recv.at[slot, slab], (cousin, dp, core),
        )

    def pass_on(slot, origin, i):
        slab = slab_of(i, half)
        landed(slot, slab)

        @pl.when(jnp.logical_and(origin < z, z < line - 1))
        def _():
            next_copy(slot, slab, 1).start()

        @pl.when(jnp.logical_and(origin > z, z > 0))
        def _():
            next_copy(slot, slab, -1).start()

        side_copy(slot, slab).start()

    length = len_ref[dp]
    cached = table_ref.shape[1] * PAGE_TOKENS
    for j in range(table_ref.shape[1]):
        page = table_ref[0, j]
        keys[j * PAGE_TOKENS:(j + 1) * PAGE_TOKENS, :] = kp_ref[page]
        values[j * PAGE_TOKENS:(j + 1) * PAGE_TOKENS, :] = vp_ref[page]
    keys[cached:, :] = fk_ref[...]
    values[cached:, :] = fv_ref[...]
    position = lax.broadcasted_iota(jnp.int32, (tokens, cached), 1)
    bias[:, :cached] = jnp.where(position < length, 0.0, MASKED)
    bias[:, cached:] = jnp.where(
        lax.broadcasted_iota(jnp.int32, (tokens, tokens), 1)
        <= lax.broadcasted_iota(jnp.int32, (tokens, tokens), 0),
        0.0, MASKED,
    )

    def act_cols(slab):
        return pl.ds(pl.multiple_of(slab * step_cols, step_cols), step_cols)

    def act_copy(i, to_peer):
        slab = core * per_core + i
        src = act.at[0, :, act_cols(slab)]
        if to_peer:
            return remote(src, act.at[1, :, act_cols(slab)], act_send.at[1, i],
                          act_recv.at[1, slab], (group, peer, core))
        return remote(src, src, act_send.at[0, i], act_recv.at[0, slab], (group, dp, other))

    def act_forward(i):
        slab = core * per_core + i
        ref = act.at[1, :, act_cols(slab)]
        return remote(ref, ref, act_fwd.at[i], act_recv.at[1, slab], (group, dp, other))

    def act_landed(block, slab):
        ref = act.at[block, :, act_cols(slab)]
        remote(ref, ref, act_fwd.at[0], act_recv.at[block, slab], (group, dp, other)).wait_recv()

    def relay(i):
        act_landed(1, core * per_core + i)
        act_forward(i).start()

    lag = 2

    def attention_step(i, carry):
        kv = (i * heads_per_step) // heads_per_kv
        kv_cols = pl.ds(pl.multiple_of(kv * HEAD_SIZE, HEAD_SIZE), HEAD_SIZE)
        for n in range(heads_per_step):
            head = i * heads_per_step + n
            q = q_ref[:, pl.ds(pl.multiple_of(head * HEAD_SIZE, HEAD_SIZE), HEAD_SIZE)]
            scores = lax.dot_general(
                q, keys[:, kv_cols], (((1,), (1,)), ((), ())), preferred_element_type=jnp.float32
            )
            scores = scores * SCALE + bias[...]
            weights = jnp.exp2(scores - jnp.max(scores, axis=-1, keepdims=True))
            total = jnp.sum(weights, axis=-1, keepdims=True)
            weighted = jnp.dot(
                weights.astype(jnp.bfloat16), values[:, kv_cols], preferred_element_type=jnp.float32
            )
            start = core * wide + head * HEAD_SIZE
            act[0, :, pl.ds(pl.multiple_of(start, HEAD_SIZE), HEAD_SIZE)] = (
                weighted / total
            ).astype(jnp.bfloat16)
        act_copy(i, True).start()
        act_copy(i, False).start()
        for side in (-1, 1):
            origin = z + side

            @pl.when(jnp.logical_and(
                jnp.logical_and(origin >= core * shards, origin < (core + 1) * shards), True))
            def _():
                pass_on(origin - core * shards, origin, i)

        @pl.when(i >= lag)
        def _():
            relay(i - lag)

        return carry

    lax.fori_loop(0, per_core, attention_step, 0)
    for i in range(per_core - lag, per_core):
        relay(i)

    def origin_of(p):
        low = core * shards
        inside = low + (z - low + p + shards * line) % shards
        return jnp.where(z < low, low + p, jnp.where(z >= low + shards, low + shards - 1 - p, inside))

    def out_cols(origin, n):
        start = (origin * 2 + y - core * 2 * shards) * cols + n * tile
        return pl.ds(pl.multiple_of(start, 128), tile)

    def out_copy(slot, n, column):
        return remote(
            stage.at[slot, n], out_ref.at[:, column], out_send.at[slot, n],
            out_recv.at[slot, n], (group, peer, core),
        )

    def product(block, slot, n):
        return jnp.dot(
            act[block], wbuf[slot, :, pl.ds(pl.multiple_of(n * tile, 128), tile)],
            preferred_element_type=jnp.float32,
        ).astype(jnp.bfloat16)

    def piece(origin, m):
        slot = origin - core * shards
        n = m % tiles
        column = out_cols(origin, n)

        @pl.when(m < tiles)
        def _():
            stage[slot, n] = product(1, slot, n)
            out_copy(slot, n, column).start()

        @pl.when(m >= tiles)
        def _():
            out_ref[:, column] = product(0, slot, n)

    def rest_landed(origin):
        slot = origin - core * shards

        def one(i, carry):
            landed(slot, slab_of(i, 1 - half))

            @pl.when(origin == z)
            def _():
                landed(slot, slab_of(i, half))

            return carry

        lax.fori_loop(0, per_core, one, 0)

    def acts_landed():
        def one(i, carry):
            act_landed(0, other * per_core + i)
            act_landed(1, other * per_core + i)
            return carry

        lax.fori_loop(0, per_core, one, 0)

    def shard_step(p, carry):
        origin = origin_of(p)
        before = origin_of(jnp.maximum(p - 1, 0))

        def chunk_step(i, inner):
            @pl.when(jnp.logical_or(origin > z + 1, origin < z - 1))
            def _():
                pass_on(origin - core * shards, origin, i)

            return inner

        lax.fori_loop(0, per_core, chunk_step, 0)

        @pl.when(p > 0)
        def _():
            @pl.when(p == 1)
            def _():
                acts_landed()

            rest_landed(before)
            lax.fori_loop(0, 2 * tiles, lambda m, inner: (piece(before, m), inner)[1], 0)

        return carry

    lax.fori_loop(0, shards, shard_step, 0)
    if shards == 1:
        acts_landed()
    last = origin_of(shards - 1)
    rest_landed(last)
    lax.fori_loop(0, 2 * tiles, lambda m, carry: (piece(last, m), carry)[1], 0)

    def finish(slot, carry):
        origin = core * shards + slot
        for n in range(tiles):
            start = (origin * 2 + 1 - y - core * 2 * shards) * cols + n * tile
            copy = out_copy(slot, n, pl.ds(pl.multiple_of(start, 128), tile))
            copy.wait_recv()
            copy.wait_send()

        @pl.when(origin != z)
        def _():
            def one(i, inner):
                slab = slab_of(i, half)

                @pl.when(jnp.logical_and(origin < z, z < line - 1))
                def _():
                    next_copy(slot, slab, 1).wait_send()

                @pl.when(jnp.logical_and(origin > z, z > 0))
                def _():
                    next_copy(slot, slab, -1).wait_send()

                side_copy(slot, slab).wait_send()
                return inner

            lax.fori_loop(0, per_core, one, 0)

        return carry

    lax.fori_loop(0, shards, finish, 0)

    def acts_sent(i, carry):
        act_copy(i, True).wait_send()
        act_copy(i, False).wait_send()
        act_forward(i).wait_send()
        return carry

    lax.fori_loop(0, per_core, acts_sent, 0)
    each_own(lambda copy: copy.wait_send())


def shards_program(line, queries, fresh_keys, fresh_values, key_pages, value_pages, table, lengths, weight):
    tokens, wide = queries.shape
    part, cols = weight.shape
    per_core = part // CHUNK
    shards = line // 2
    tile = min(cols, 256)
    tiles = cols // tile
    span = table.shape[1] * PAGE_TOKENS + tokens
    kv_width = fresh_keys.shape[1]
    out_width = 2 * shards * cols
    vmem = pl.BlockSpec(memory_space=pltpu.VMEM)
    smem = pl.BlockSpec(memory_space=pltpu.SMEM)
    dma = pltpu.SemaphoreType.DMA
    heads = wide // HEAD_SIZE
    flops = 4 * heads * tokens * span * HEAD_SIZE + 2 * 2 * tokens * 2 * part * shards * cols
    return pl.pallas_call(
        functools.partial(kernel, line),
        out_shape=jax.ShapeDtypeStruct((tokens, out_width), jnp.bfloat16),
        in_specs=[vmem, vmem, vmem, vmem, vmem, smem, smem, pl.BlockSpec(memory_space=pl.ANY)],
        out_specs=vmem,
        scratch_shapes=[
            pltpu.VMEM((shards, 2 * part, cols), jnp.bfloat16),
            pltpu.VMEM((2, tokens, 2 * wide), jnp.bfloat16),
            pltpu.VMEM((shards, tiles, tokens, tile), jnp.bfloat16),
            pltpu.VMEM((span, kv_width), jnp.bfloat16),
            pltpu.VMEM((span, kv_width), jnp.bfloat16),
            pltpu.VMEM((tokens, span), jnp.float32),
            dma((shards, 2 * per_core)),
            dma((shards, 2 * per_core)),
            dma((shards, 2 * per_core)),
            dma((3, per_core)),
            dma((2, 2 * per_core)),
            dma((2, per_core)),
            dma((per_core,)),
            dma((shards, tiles)),
            dma((shards, tiles)),
        ],
        compiler_params=pltpu.CompilerParams(
            collective_id=0, has_side_effects=True, vmem_limit_bytes=60 * 1024 * 1024
        ),
        cost_estimate=pl.CostEstimate(
            flops=flops, bytes_accessed=8 * 1024 * 1024, transcendentals=heads * tokens * span
        ),
    )(queries, fresh_keys, fresh_values, key_pages, value_pages, table, lengths, weight)


def solution(mesh):
    return jax.shard_map(
        functools.partial(shards_program, mesh.shape["dp"] // 2),
        mesh=mesh,
        in_specs=(
            P(("groups", "dp"), "tensor"),
            P(("groups", "dp"), "tensor"),
            P(("groups", "dp"), "tensor"),
            P(("groups", "dp"), None, "tensor"),
            P(("groups", "dp"), None, "tensor"),
            P(("groups", "dp"), None),
            P("groups"),
            P("tensor", "dp"),
        ),
        out_specs=P(("groups", "dp"), "tensor"),
        check_vma=False,
    )
```

profile of v0, /device:TPU:1, one launch (start us, length us, event | category | flops | bytes accessed | tf_op | source)
XLA Modules:
  0.0 94.4 jit_solution(5732694691598888475)
XLA Ops:
  0.0 92.1 %shard_map.82 = bf16[256,2048]{1,0:T(8,128)(2,1)} custom-call(bf16[256,2048]{1,0:T(8,128)(2,1)} %q_ref.1, bf16[256,256]{1,0:T(8,128)(2,1)} %fk_ref.1, bf16[256,256]{1,0:T(8,128)(2,1)} %fv_ref.1, bf16[10,128,256]{2,1,0:T(8,128)(2,1)} %kp_ref.1, bf16[10,128,256]{2,1,0:T(8,128)(2,1)} %vp_ref.1, s32[1,8]{1,0:T(1,128)} %table_ref.1, s32[8]{0:T(128)} %len_ref.1, ...), custom_call_target="tpu_custom_call" | custom-call | flops 6979321856 | bytes 8388608 | tf_op jit(solution)/shard_map/pallas_call | solution.py:373
  92.1 2.3 %copy.10 = bf16[256,2048]{1,0:T(8,128)(2,1)} copy(bf16[256,2048]{1,0:T(8,128)(2,1)} %shard_map.82) | data formatting | bytes 2097152
where the time goes:
time: 94.6 us; the launch traced here: 94.4 us
  Pallas kernels  92.1 us (97%)
  local copies, waits for them, and re-layouts  2.3 us (2%)
    pallas_call x1, Pallas kernels, shards_program(): pl.pallas_call(functools.partial(kernel, line), out_shape=jax.ShapeDtypeS...  92.1 us
    unnamed x1, local copies, waits for them, and re-layouts  2.3 us

commit v1 on v0

--- a/solution.py
+++ b/solution.py
@@ -11,6 +11,8 @@
 QUERY_GROUP = 8
 PAGE_TOKENS = 128
 CHUNK = 256
+OUTER_ZY = 7
+INNER_ZY = 5
 SCALE = HEAD_SIZE ** (-0.5) * 1.4426950408889634
 MASKED = -1e30
 
@@ -401,9 +403,425 @@
     )(queries, fresh_keys, fresh_values, key_pages, value_pages, table, lengths, weight)
 
 
+def square_kernel(
+    line, q_ref, fk_ref, fv_ref, kp_ref, vp_ref, table_ref, len_ref, w_ref, out_ref,
+    act, wall, relay, px_out, px_in, keep, stage, keys, values, bias,
+    w_recv, w_send, w_side, r_recv, own_sem, act_recv, act_send, act_fwd,
+    px_recv, px_send, out_recv, out_send,
+):
+    group, dp, core = lax.axis_index("groups"), lax.axis_index("dp"), lax.axis_index("tensor")
+    z, y = dp // 2, dp % 2
+    x = group % 2
+    cousin = group + 1 - 2 * x
+    other = 1 - core
+    half = z // 2
+    inner = z % 2 != half
+    outer = jnp.logical_not(inner)
+    zp = z + 1 - 2 * (z % 2)
+    zm = jnp.where(inner, line - 1 - z, z)
+    peer = z * 2 + 1 - y
+    part, cols = w_ref.shape
+    tokens, wide = q_ref.shape
+    chunks = part // CHUNK
+    unit = cols // 2
+    rows_mine = tokens // 2
+    steps = wide // 256
+    step_cols = wide // steps
+    heads_per_step = step_cols // HEAD_SIZE
+    near, far = steps * OUTER_ZY // 8, steps * INNER_ZY // 8
+    first = min(2, chunks)
+
+    def remote(src, dst, send, recv, where):
+        return pltpu.make_async_remote_copy(
+            src_ref=src, dst_ref=dst, send_sem=send, recv_sem=recv,
+            device_id=where, device_id_type=pl.DeviceIdType.MESH,
+        )
+
+    def loop(low, high, act_on):
+        lax.fori_loop(low, high, lambda k, carry: (act_on(k), carry)[1], 0)
+
+    def rows(k):
+        return pl.ds(pl.multiple_of(k * CHUNK, CHUNK), CHUNK)
+
+    barrier = pltpu.get_barrier_semaphore()
+
+    def greet(where):
+        pl.semaphore_signal(barrier, inc=1, device_id=where, device_id_type=pl.DeviceIdType.MESH)
+
+    greet((group, dp, other))
+    for chip in (peer, zp * 2 + y, zp * 2 + 1 - y):
+        greet((group, chip, core))
+        greet((group, chip, other))
+
+    @pl.when(inner)
+    def _():
+        greet((cousin, dp, core))
+        greet((group, zm * 2 + y, core))
+
+    pl.semaphore_wait(barrier, 7 + jnp.where(inner, 2, 0))
+
+    half_cols = pl.ds(pl.multiple_of(x * unit, 128), unit)
+
+    def mid_own(k):
+        return remote(
+            w_ref.at[rows(k), half_cols], wall.at[1, x, rows(k)],
+            w_send.at[0, k], w_recv.at[0, x, k], (group, zm * 2 + y, core),
+        )
+
+    def to_relay(k):
+        return remote(
+            w_ref.at[rows(k), half_cols], relay.at[rows(k)],
+            w_send.at[0, k], r_recv.at[k], (group, zp * 2 + y, core),
+        )
+
+    def mid_relay(k):
+        return remote(
+            relay.at[rows(k)], wall.at[2, x, rows(k)],
+            w_send.at[1, k], w_recv.at[1, x, k], (group, zm * 2 + y, core),
+        )
+
+    def side(s, k):
+        ref = wall.at[s, x, rows(k)]
+        return remote(ref, ref, w_side.at[s - 1, k], w_recv.at[s - 1, x, k], (cousin, dp, core))
+
+    def w_landed(s, u, k):
+        ref = wall.at[s, u, rows(k)]
+        remote(ref, ref, w_side.at[s - 1, k], w_recv.at[s - 1, u, k], (cousin, dp, core)).wait_recv()
+
+    def relay_on(k):
+        to_relay(k).wait_recv()
+        mid_relay(k).start()
+
+    def side_on(s, k):
+        w_landed(s, x, k)
+        side(s, k).start()
+
+    def own_copy(u):
+        return pltpu.make_async_copy(
+            w_ref.at[:, u * unit:(u + 1) * unit], wall.at[0, u], own_sem.at[u]
+        )
+
+    @pl.when(inner)
+    def _():
+        loop(0, chunks, lambda k: mid_own(k).start())
+
+    @pl.when(outer)
+    def _():
+        loop(0, first, lambda k: to_relay(k).start())
+
+    own_copy(0).start()
+    own_copy(1).start()
+
+    length = len_ref[dp]
+    cached = table_ref.shape[1] * PAGE_TOKENS
+    for j in range(table_ref.shape[1]):
+        page = table_ref[0, j]
+        keys[j * PAGE_TOKENS:(j + 1) * PAGE_TOKENS, :] = kp_ref[page]
+        values[j * PAGE_TOKENS:(j + 1) * PAGE_TOKENS, :] = vp_ref[page]
+    keys[cached:, :] = fk_ref[...]
+    values[cached:, :] = fv_ref[...]
+    position = lax.broadcasted_iota(jnp.int32, (tokens, cached), 1)
+    bias[:, :cached] = jnp.where(position < length, 0.0, MASKED)
+    bias[:, cached:] = jnp.where(
+        lax.broadcasted_iota(jnp.int32, (tokens, tokens), 1)
+        <= lax.broadcasted_iota(jnp.int32, (tokens, tokens), 0),
+        0.0, MASKED,
+    )
+
+    def act_at(slot, i):
+        return act.at[slot, :, pl.ds(pl.multiple_of(i * step_cols, step_cols), step_cols)]
+
+    def act_y(i):
+        return remote(act_at(0, i), act_at(1, i), act_send.at[0, i], act_recv.at[0, i],
+                      (group, peer, core))
+
+    def act_z(i):
+        return remote(act_at(0, i), act_at(2, i), act_send.at[1, i], act_recv.at[1, i],
+                      (group, zp * 2 + y, core))
+
+    def on_y(i):
+        return remote(act_at(2, i), act_at(3, i), act_fwd.at[0, i], act_recv.at[2, i],
+                      (group, peer, core))
+
+    def on_z(i):
+        return remote(act_at(1, i), act_at(3, i), act_fwd.at[1, i], act_recv.at[2, i],
+                      (group, zp * 2 + y, core))
+
+    over_y = jnp.where(inner, near, far)
+    over_z = jnp.where(inner, far, near)
+
+    def act_on(i):
+        act_y(i).wait_recv()
+
+        @pl.when(i >= over_z)
+        def _():
+            on_z(i).start()
+
+        act_z(i).wait_recv()
+
+        @pl.when(i < over_y)
+        def _():
+            on_y(i).start()
+
+    lag = 2
+
+    def attention_step(i):
+        kv = (i * heads_per_step) // QUERY_GROUP
+        kv_cols = pl.ds(pl.multiple_of(kv * HEAD_SIZE, HEAD_SIZE), HEAD_SIZE)
+        for n in range(heads_per_step):
+            start = pl.multiple_of((i * heads_per_step + n) * HEAD_SIZE, HEAD_SIZE)
+            q = q_ref[:, pl.ds(start, HEAD_SIZE)]
+            scores = lax.dot_general(
+                q, keys[:, kv_cols], (((1,), (1,)), ((), ())), preferred_element_type=jnp.float32
+            )
+            scores = scores * SCALE + bias[...]
+            weights = jnp.exp2(scores - jnp.max(scores, axis=-1, keepdims=True))
+            total = jnp.sum(weights, axis=-1, keepdims=True)
+            weighted = jnp.dot(
+                weights.astype(jnp.bfloat16), values[:, kv_cols], preferred_element_type=jnp.float32
+            )
+            act[0, :, pl.ds(start, HEAD_SIZE)] = (weighted / total).astype(jnp.bfloat16)
+        act_y(i).start()
+        act_z(i).start()
+
+        @pl.when(i >= lag)
+        def _():
+            act_on(i - lag)
+
+            @pl.when(inner)
+            def _():
+                side_on(1, i - lag)
+
+    loop(0, steps, attention_step)
+
+    @pl.when(outer)
+    def _():
+        loop(first, chunks, lambda k: to_relay(k).start())
+
+    def shard_z(s):
+        return jnp.where(s == 0, z, jnp.where(s == 1, zm, (line - 1) * (1 - half)))
+
+    def task(s, u, slot):
+        return (s * 2 + u) * 4 + slot
+
+    def swap(t):
+        return remote(px_out.at[t], px_in.at[t], px_send.at[t], px_recv.at[t], (group, dp, other))
+
+    def place(s, u):
+        zs = shard_z(s)
+        to = zs // 2
+        column = (zs * 2 + y - to * line) * cols + u * unit
+        spot = ((zs % 2) * 2 + y) * 4 + u * 2 + core
+        ref = out_ref.at[pl.ds(pl.multiple_of(core * rows_mine, rows_mine), rows_mine),
+                         pl.ds(pl.multiple_of(column, 128), unit)]
+        return to, ref, spot
+
+    def out_copy(s, u, slot):
+        to, ref, spot = place(s, u)
+        t = task(s, u, slot)
+        zd = jnp.where(slot >= 2, zp, z)
+        yd = jnp.where(slot % 2 == 1, 1 - y, y)
+        return remote(stage.at[t], ref, out_send.at[t], out_recv.at[spot], (group, zd * 2 + yd, to))
+
+    def stays(s, slot):
+        return jnp.logical_and(slot == 0, shard_z(s) // 2 == core)
+
+    def begin(s, u, slot):
+        t = task(s, u, slot)
+        keep[t] = jnp.dot(act[slot], wall[s, u], preferred_element_type=jnp.float32)
+        start = pl.multiple_of(other * rows_mine, rows_mine)
+        px_out[t] = keep[t, pl.ds(start, rows_mine), :].astype(jnp.bfloat16)
+        swap(t).start()
+
+    def finish(s, u, slot):
+        t = task(s, u, slot)
+        swap(t).wait_recv()
+        start = pl.multiple_of(core * rows_mine, rows_mine)
+        stage[t] = (keep[t, pl.ds(start, rows_mine), :] + px_in[t].astype(jnp.float32)).astype(jnp.bfloat16)
+
+        @pl.when(stays(s, slot))
+        def _():
+            to, ref, spot = place(s, u)
+            pltpu.make_async_copy(stage.at[t], ref, out_recv.at[spot]).start()
+
+        @pl.when(jnp.logical_not(stays(s, slot)))
+        def _():
+            out_copy(s, u, slot).start()
+
+    def run(low, high, which):
+        def one(n):
+            begin(*which(n))
+
+            @pl.when(n > low)
+            def _():
+                finish(*which(n - 1))
+
+        loop(low, high, one)
+
+    loop(steps - lag, steps, act_on)
+    own_copy(0).wait()
+    own_copy(1).wait()
+
+    def corner_landed():
+        loop(0, steps, lambda i: on_y(i).wait_recv())
+
+    @pl.when(outer)
+    def _():
+        def which(n):
+            return 0, n % 2, n // 2
+
+        run(0, 6, which)
+        corner_landed()
+        finish(*which(5))
+        run(6, 8, which)
+        finish(*which(7))
+
+    @pl.when(inner)
+    def _():
+        loop(steps - lag, chunks, lambda k: side_on(1, k))
+        loop(0, first, relay_on)
+        loop(0, chunks, lambda k: w_landed(1, 1 - x, k))
+
+        def which(n):
+            return (n % 4) // 2, n % 2, n // 4
+
+        per = 12 // (chunks - first)
+
+        def mixed(k):
+            relay_on(k)
+            for m in range(per):
+                n = (k - first) * per + m
+                begin(*which(n))
+
+                @pl.when(n > 0)
+                def _():
+                    finish(*which(n - 1))
+
+            side_on(2, k - first)
+
+        loop(first, chunks, mixed)
+        run(per * (chunks - first), 12, which)
+        finish(*which(11))
+        loop(chunks - first, chunks - 1, lambda k: side_on(2, k))
+        corner_landed()
+        run(12, 16, which)
+        finish(*which(15))
+        side_on(2, chunks - 1)
+
+        def last(n):
+            return 2, jnp.where(n < 4, x, 1 - x), n % 4
+
+        run(0, 4, last)
+        loop(0, chunks, lambda k: w_landed(2, 1 - x, k))
+        finish(*last(3))
+        run(4, 8, last)
+        finish(*last(7))
+
+    def drain(t):
+        swap(t).wait_send()
+        s, u, slot = t // 8, (t // 4) % 2, t % 4
+
+        @pl.when(jnp.logical_not(stays(s, slot)))
+        def _():
+            out_copy(s, u, slot).wait_send()
+
+    loop(0, jnp.where(inner, 24, 8), drain)
+
+    def act_sent(i):
+        act_y(i).wait_send()
+        act_z(i).wait_send()
+
+        @pl.when(i >= over_z)
+        def _():
+            on_z(i).wait_send()
+
+        @pl.when(i < over_y)
+        def _():
+            on_y(i).wait_send()
+
+    loop(0, steps, act_sent)
+
+    def weight_sent(k):
+        @pl.when(outer)
+        def _():
+            to_relay(k).wait_send()
+
+        @pl.when(inner)
+        def _():
+            mid_own(k).wait_send()
+            mid_relay(k).wait_send()
+            side(1, k).wait_send()
+            side(2, k).wait_send()
+
+    loop(0, chunks, weight_sent)
+
+    def out_landed(n):
+        column = pl.ds(pl.multiple_of((n // 2) * unit, 128), unit)
+        ref = out_ref.at[pl.ds(pl.multiple_of((n % 2) * rows_mine, rows_mine), rows_mine), column]
+        remote(stage.at[0], ref, out_send.at[0], out_recv.at[n], (group, dp, other)).wait_recv()
+
+    loop(0, 16, out_landed)
+
+
+def square_program(line, queries, fresh_keys, fresh_values, key_pages, value_pages, table, lengths, weight):
+    tokens, wide = queries.shape
+    part, cols = weight.shape
+    chunks = part // CHUNK
+    steps = wide // 256
+    unit = cols // 2
+    span = table.shape[1] * PAGE_TOKENS + tokens
+    kv_width = fresh_keys.shape[1]
+    vmem = pl.BlockSpec(memory_space=pltpu.VMEM)
+    smem = pl.BlockSpec(memory_space=pltpu.SMEM)
+    dma = pltpu.SemaphoreType.DMA
+    bf16, f32 = jnp.bfloat16, jnp.float32
+    heads = wide // HEAD_SIZE
+    flops = 4 * heads * tokens * span * HEAD_SIZE + 2 * 24 * tokens * part * unit
+    return pl.pallas_call(
+        functools.partial(square_kernel, line),
+        out_shape=jax.ShapeDtypeStruct((tokens, line * cols), bf16),
+        in_specs=[vmem, vmem, vmem, vmem, vmem, smem, smem, pl.BlockSpec(memory_space=pl.ANY)],
+        out_specs=vmem,
+        scratch_shapes=[
+            pltpu.VMEM((4, tokens, wide), bf16),
+            pltpu.VMEM((3, 2, part, unit), bf16),
+            pltpu.VMEM((part, unit), bf16),
+            pltpu.VMEM((24, tokens // 2, unit), bf16),
+            pltpu.VMEM((24, tokens // 2, unit), bf16),
+            pltpu.VMEM((24, tokens, unit), f32),
+            pltpu.VMEM((24, tokens // 2, unit), bf16),
+            pltpu.VMEM((span, kv_width), bf16),
+            pltpu.VMEM((span, kv_width), bf16),
+            pltpu.VMEM((tokens, span), f32),
+            dma((2, 2, chunks)),
+            dma((2, chunks)),
+            dma((2, chunks)),
+            dma((chunks,)),
+            dma((2,)),
+            dma((3, steps)),
+            dma((2, steps)),
+            dma((2, steps)),
+            dma((24,)),
+            dma((24,)),
+            dma((16,)),
+            dma((24,)),
+        ],
+        compiler_params=pltpu.CompilerParams(
+            collective_id=0, has_side_effects=True, vmem_limit_bytes=60 * 1024 * 1024
+        ),
+        cost_estimate=pl.CostEstimate(
+            flops=flops, bytes_accessed=8 * 1024 * 1024, transcendentals=heads * tokens * span
+        ),
+    )(queries, fresh_keys, fresh_values, key_pages, value_pages, table, lengths, weight)
+
+
+def program_of(line):
+    return square_program if line == 4 else shards_program
+
+
 def solution(mesh):
     return jax.shard_map(
-        functools.partial(shards_program, mesh.shape["dp"] // 2),
+        functools.partial(program_of(mesh.shape["dp"] // 2), mesh.shape["dp"] // 2),
         mesh=mesh,
         in_specs=(
             P(("groups", "dp"), "tensor"),

time: 94.6 us -> 92.1 us (0.974)
  Pallas kernels: 92.1 us -> 89.6 us
    pallas_call x1, Pallas kernels: 92.1 us -> 89.6 us  [square_program(): pl.pallas_call(functools.partial(square_kernel, line), out_shape=jax.Shap...]
where the time goes in v1:
time: 92.1 us; the launch traced here: 92 us
  Pallas kernels  89.6 us (97%)
  local copies, waits for them, and re-layouts  2.3 us (2%)
    pallas_call x1, Pallas kernels, square_program(): pl.pallas_call(functools.partial(square_kernel, line), out_shape=jax.Shap...  89.6 us
    unnamed x1, local copies, waits for them, and re-layouts  2.3 us

profile of v1, /device:TPU:1, one launch (start us, length us, event | category | flops | bytes accessed | tf_op | source)
XLA Modules:
  0.0 92.0 jit_solution(6711841754092151418)
XLA Ops:
  0.0 89.6 %shard_map.82 = bf16[256,2048]{1,0:T(8,128)(2,1)} custom-call(bf16[256,2048]{1,0:T(8,128)(2,1)} %q_ref.1, bf16[256,256]{1,0:T(8,128)(2,1)} %fk_ref.1, bf16[256,256]{1,0:T(8,128)(2,1)} %fv_ref.1, bf16[10,128,256]{2,1,0:T(8,128)(2,1)} %kp_ref.1, bf16[10,128,256]{2,1,0:T(8,128)(2,1)} %vp_ref.1, s32[1,8]{1,0:T(1,128)} %table_ref.1, s32[8]{0:T(128)} %len_ref.1, ...), custom_call_target="tpu_custom_call" | custom-call | flops 9126805504 | bytes 8388608 | tf_op jit(solution)/shard_map/pallas_call | solution.py:780
  89.7 2.3 %copy.10 = bf16[256,2048]{1,0:T(8,128)(2,1)} copy(bf16[256,2048]{1,0:T(8,128)(2,1)} %shard_map.82) | data formatting | bytes 2097152

commit v2 on v1

--- a/solution.py
+++ b/solution.py
@@ -404,10 +404,11 @@
 
 
 def square_kernel(
-    line, q_ref, fk_ref, fv_ref, kp_ref, vp_ref, table_ref, len_ref, w_ref, out_ref,
-    act, wall, relay, px_out, px_in, keep, stage, keys, values, bias,
-    w_recv, w_send, w_side, r_recv, own_sem, act_recv, act_send, act_fwd,
-    px_recv, px_send, out_recv, out_send,
+    line, q_hbm, fk_hbm, fv_hbm, kp_hbm, vp_hbm, table_ref, len_ref, w_ref, out_ref,
+    q_ref, kp_ref, vp_ref, act, wall, relay, px_out, px_in, keep, stage, keys, values, bias,
+    w_recv, w_swap, w_send, r_recv, own_sem, act_recv, act_send,
+    px_recv, px_send, out_recv, out_send, in_sem,
+    far_out, far_in, far_keep, far_stage, far_recv,
 ):
     group, dp, core = lax.axis_index("groups"), lax.axis_index("dp"), lax.axis_index("tensor")
     z, y = dp // 2, dp % 2
@@ -424,12 +425,13 @@
     tokens, wide = q_ref.shape
     chunks = part // CHUNK
     unit = cols // 2
+    lane = unit // 2
+    tall = 2 * CHUNK
     rows_mine = tokens // 2
     steps = wide // 256
     step_cols = wide // steps
     heads_per_step = step_cols // HEAD_SIZE
     near, far = steps * OUTER_ZY // 8, steps * INNER_ZY // 8
-    first = min(2, chunks)
 
     def remote(src, dst, send, recv, where):
         return pltpu.make_async_remote_copy(
@@ -443,6 +445,18 @@
     def rows(k):
         return pl.ds(pl.multiple_of(k * CHUNK, CHUNK), CHUNK)
 
+    cached = table_ref.shape[1] * PAGE_TOKENS
+
+    loads = [
+        pltpu.make_async_copy(kp_hbm, kp_ref, in_sem.at[0]),
+        pltpu.make_async_copy(vp_hbm, vp_ref, in_sem.at[1]),
+        pltpu.make_async_copy(fk_hbm, keys.at[cached:], in_sem.at[2]),
+        pltpu.make_async_copy(fv_hbm, values.at[cached:], in_sem.at[3]),
+        pltpu.make_async_copy(q_hbm, q_ref, in_sem.at[4]),
+    ]
+    for copy in loads:
+        copy.start()
+
     barrier = pltpu.get_barrier_semaphore()
 
     def greet(where):
@@ -461,39 +475,52 @@
     pl.semaphore_wait(barrier, 7 + jnp.where(inner, 2, 0))
 
     half_cols = pl.ds(pl.multiple_of(x * unit, 128), unit)
+    deep = chunks // 2
+
+    def patch(k):
+        return (pl.ds(pl.multiple_of(k % deep * tall, tall), tall),
+                pl.ds(pl.multiple_of(k // deep * lane, 128), lane))
 
     def mid_own(k):
         return remote(
             w_ref.at[rows(k), half_cols], wall.at[1, x, rows(k)],
-            w_send.at[0, k], w_recv.at[0, x, k], (group, zm * 2 + y, core),
+            w_send.at[0], w_recv.at[0, k], (group, zm * 2 + y, core),
         )
 
     def to_relay(k):
         return remote(
-            w_ref.at[rows(k), half_cols], relay.at[rows(k)],
-            w_send.at[0, k], r_recv.at[k], (group, zp * 2 + y, core),
+            w_ref.at[patch(k)[0], pl.ds(pl.multiple_of(x * unit + k // deep * lane, 128), lane)], relay.at[patch(k)],
+            w_send.at[0], r_recv.at[k], (group, zp * 2 + y, core),
         )
 
     def mid_relay(k):
         return remote(
-            relay.at[rows(k)], wall.at[2, x, rows(k)],
-            w_send.at[1, k], w_recv.at[1, x, k], (group, zm * 2 + y, core),
+            relay.at[patch(k)], wall.at[2, x, *patch(k)],
+            w_send.at[1], w_recv.at[1, k], (group, zm * 2 + y, core),
         )
 
     def side(s, k):
-        ref = wall.at[s, x, rows(k)]
-        return remote(ref, ref, w_side.at[s - 1, k], w_recv.at[s - 1, x, k], (cousin, dp, core))
-
-    def w_landed(s, u, k):
-        ref = wall.at[s, u, rows(k)]
-        remote(ref, ref, w_side.at[s - 1, k], w_recv.at[s - 1, u, k], (cousin, dp, core)).wait_recv()
+        if s == 1:
+            ref, sem = wall.at[s, x, rows(k)], w_swap.at[0]
+        else:
+            ref, sem = wall.at[s, x, *patch(k)], w_swap.at[1 + k // deep]
+        return remote(ref, ref, w_send.at[s + 1], sem, (cousin, dp, core))
+
+    def swapped(ref, n):
+        remote(ref, ref, w_send.at[2], w_swap.at[n], (cousin, dp, core)).wait_recv()
+
+    def near_swapped():
+        swapped(wall.at[1, 1 - x], 0)
+
+    def far_swapped(v):
+        swapped(wall.at[2, 1 - x, :, v * lane:(v + 1) * lane], 1 + v)
 
     def relay_on(k):
         to_relay(k).wait_recv()
         mid_relay(k).start()
 
     def side_on(s, k):
-        w_landed(s, x, k)
+        (mid_own(k) if s == 1 else mid_relay(k)).wait_recv()
         side(s, k).start()
 
     def own_copy(u):
@@ -507,19 +534,12 @@
 
     @pl.when(outer)
     def _():
-        loop(0, first, lambda k: to_relay(k).start())
+        to_relay(0).start()
 
     own_copy(0).start()
     own_copy(1).start()
 
     length = len_ref[dp]
-    cached = table_ref.shape[1] * PAGE_TOKENS
-    for j in range(table_ref.shape[1]):
-        page = table_ref[0, j]
-        keys[j * PAGE_TOKENS:(j + 1) * PAGE_TOKENS, :] = kp_ref[page]
-        values[j * PAGE_TOKENS:(j + 1) * PAGE_TOKENS, :] = vp_ref[page]
-    keys[cached:, :] = fk_ref[...]
-    values[cached:, :] = fv_ref[...]
     position = lax.broadcasted_iota(jnp.int32, (tokens, cached), 1)
     bias[:, :cached] = jnp.where(position < length, 0.0, MASKED)
     bias[:, cached:] = jnp.where(
@@ -527,43 +547,48 @@
         <= lax.broadcasted_iota(jnp.int32, (tokens, tokens), 0),
         0.0, MASKED,
     )
+    for copy in loads:
+        copy.wait()
+    for j in range(table_ref.shape[1]):
+        page = table_ref[0, j]
+        keys[j * PAGE_TOKENS:(j + 1) * PAGE_TOKENS, :] = kp_ref[page]
+        values[j * PAGE_TOKENS:(j + 1) * PAGE_TOKENS, :] = vp_ref[page]
 
     def act_at(slot, i):
         return act.at[slot, :, pl.ds(pl.multiple_of(i * step_cols, step_cols), step_cols)]
 
     def act_y(i):
-        return remote(act_at(0, i), act_at(1, i), act_send.at[0, i], act_recv.at[0, i],
+        return remote(act_at(0, i), act_at(1, i), act_send.at[0], act_recv.at[1, i],
                       (group, peer, core))
 
     def act_z(i):
-        return remote(act_at(0, i), act_at(2, i), act_send.at[1, i], act_recv.at[1, i],
+        return remote(act_at(0, i), act_at(2, i), act_send.at[1], act_recv.at[0, i],
                       (group, zp * 2 + y, core))
 
     def on_y(i):
-        return remote(act_at(2, i), act_at(3, i), act_fwd.at[0, i], act_recv.at[2, i],
+        return remote(act_at(2, i), act_at(3, i), act_send.at[2], act_recv.at[1, steps],
                       (group, peer, core))
 
     def on_z(i):
-        return remote(act_at(1, i), act_at(3, i), act_fwd.at[1, i], act_recv.at[2, i],
+        return remote(act_at(1, i), act_at(3, i), act_send.at[3], act_recv.at[1, steps],
                       (group, zp * 2 + y, core))
 
     over_y = jnp.where(inner, near, far)
     over_z = jnp.where(inner, far, near)
 
-    def act_on(i):
+    def from_y(i):
         act_y(i).wait_recv()
 
         @pl.when(i >= over_z)
         def _():
             on_z(i).start()
 
+    def from_z(i):
         act_z(i).wait_recv()
 
         @pl.when(i < over_y)
         def _():
             on_y(i).start()
-
-    lag = 2
 
     def attention_step(i):
         kv = (i * heads_per_step) // QUERY_GROUP
@@ -584,44 +609,47 @@
         act_y(i).start()
         act_z(i).start()
 
-        @pl.when(i >= lag)
-        def _():
-            act_on(i - lag)
-
-            @pl.when(inner)
-            def _():
-                side_on(1, i - lag)
+        @pl.when(jnp.logical_and(outer, i % 2 == 1))
+        def _():
+            to_relay((i + 1) // 2).start()
+
+        @pl.when(jnp.logical_and(inner, jnp.logical_and(i >= 3, i % 2 == 1)))
+        def _():
+            side_on(1, (i - 3) // 2)
+
+        @pl.when(jnp.logical_and(inner, i == 3))
+        def _():
+            relay_on(0)
 
     loop(0, steps, attention_step)
 
     @pl.when(outer)
     def _():
-        loop(first, chunks, lambda k: to_relay(k).start())
+        loop(steps // 2 + 1, chunks, lambda k: to_relay(k).start())
 
     def shard_z(s):
-        return jnp.where(s == 0, z, jnp.where(s == 1, zm, (line - 1) * (1 - half)))
+        return jnp.where(s == 0, z, zm)
 
     def task(s, u, slot):
         return (s * 2 + u) * 4 + slot
 
     def swap(t):
-        return remote(px_out.at[t], px_in.at[t], px_send.at[t], px_recv.at[t], (group, dp, other))
+        return remote(px_out.at[t], px_in.at[t], px_send.at[0], px_recv.at[t], (group, dp, other))
 
     def place(s, u):
         zs = shard_z(s)
         to = zs // 2
         column = (zs * 2 + y - to * line) * cols + u * unit
-        spot = ((zs % 2) * 2 + y) * 4 + u * 2 + core
         ref = out_ref.at[pl.ds(pl.multiple_of(core * rows_mine, rows_mine), rows_mine),
                          pl.ds(pl.multiple_of(column, 128), unit)]
-        return to, ref, spot
+        return to, ref
 
     def out_copy(s, u, slot):
-        to, ref, spot = place(s, u)
+        to, ref = place(s, u)
         t = task(s, u, slot)
         zd = jnp.where(slot >= 2, zp, z)
         yd = jnp.where(slot % 2 == 1, 1 - y, y)
-        return remote(stage.at[t], ref, out_send.at[t], out_recv.at[spot], (group, zd * 2 + yd, to))
+        return remote(stage.at[t], ref, out_send.at[0], out_recv.at[0], (group, zd * 2 + yd, to))
 
     def stays(s, slot):
         return jnp.logical_and(slot == 0, shard_z(s) // 2 == core)
@@ -641,126 +669,179 @@
 
         @pl.when(stays(s, slot))
         def _():
-            to, ref, spot = place(s, u)
-            pltpu.make_async_copy(stage.at[t], ref, out_recv.at[spot]).start()
+            to, ref = place(s, u)
+            pltpu.make_async_copy(stage.at[t], ref, out_recv.at[0]).start()
 
         @pl.when(jnp.logical_not(stays(s, slot)))
         def _():
             out_copy(s, u, slot).start()
 
-    def run(low, high, which):
-        def one(n):
-            begin(*which(n))
-
-            @pl.when(n > low)
-            def _():
-                finish(*which(n - 1))
-
-        loop(low, high, one)
-
-    loop(steps - lag, steps, act_on)
+    def strip(w):
+        return jnp.where(w % 2 == 0, x, 1 - x), w // 2
+
+    def far_swap(w, p):
+        pair = pl.ds(p * 2, 2)
+        return remote(far_out.at[w, pair], far_in.at[w, pair], px_send.at[1], far_recv.at[w, p],
+                      (group, dp, other))
+
+    def far_begin(w, p):
+        u, v = strip(w)
+        pair = pl.ds(p * 2, 2)
+        far_keep[w, pair] = jnp.dot(
+            act[pair].reshape(2 * tokens, wide), wall[2, u, :, pl.ds(pl.multiple_of(v * lane, 128), lane)],
+            preferred_element_type=jnp.float32,
+        ).reshape(2, tokens, lane)
+        start = pl.multiple_of(other * rows_mine, rows_mine)
+        far_out[w, pair] = far_keep[w, pair, pl.ds(start, rows_mine), :].astype(jnp.bfloat16)
+        far_swap(w, p).start()
+
+    def far_place(w):
+        u, v = strip(w)
+        zs = (line - 1) * (1 - half)
+        to = zs // 2
+        column = (zs * 2 + y - to * line) * cols + u * unit + v * lane
+        ref = out_ref.at[pl.ds(pl.multiple_of(core * rows_mine, rows_mine), rows_mine),
+                         pl.ds(pl.multiple_of(column, 128), lane)]
+        return to, ref
+
+    def far_copy(w, slot):
+        to, ref = far_place(w)
+        zd = jnp.where(slot >= 2, zp, z)
+        yd = jnp.where(slot % 2 == 1, 1 - y, y)
+        return remote(far_stage.at[w, slot], ref, out_send.at[1], out_recv.at[0], (group, zd * 2 + yd, to))
+
+    def far_stays(slot):
+        return jnp.logical_and(slot == 0, 1 - half == core)
+
+    def far_finish(w, p):
+        far_swap(w, p).wait_recv()
+        pair = pl.ds(p * 2, 2)
+        start = pl.multiple_of(core * rows_mine, rows_mine)
+        far_stage[w, pair] = (
+            far_keep[w, pair, pl.ds(start, rows_mine), :] + far_in[w, pair].astype(jnp.float32)
+        ).astype(jnp.bfloat16)
+        far_copy(w, p * 2 + 1).start()
+
+        @pl.when(far_stays(p * 2))
+        def _():
+            to, ref = far_place(w)
+            pltpu.make_async_copy(far_stage.at[w, p * 2], ref, out_recv.at[0]).start()
+
+        @pl.when(jnp.logical_not(far_stays(p * 2)))
+        def _():
+            far_copy(w, p * 2).start()
+
     own_copy(0).wait()
     own_copy(1).wait()
 
+    def run(count, kinds, duties):
+        def each(n, what):
+            for holds, which, acts in kinds:
+                @pl.when(holds(n))
+                def _():
+                    acts[what](*which(n))
+
+        def one(n):
+            for at, todo in duties.items():
+                @pl.when(n == at)
+                def _():
+                    for act_now in todo:
+                        act_now()
+
+            @pl.when(n < count)
+            def _():
+                each(n, 0)
+
+            @pl.when(n > 0)
+            def _():
+                each(n - 1, 1)
+
+        loop(0, count + 1, one)
+
     def corner_landed():
-        loop(0, steps, lambda i: on_y(i).wait_recv())
+        remote(act.at[2], act.at[3], act_send.at[2], act_recv.at[1, steps], (group, peer, core)).wait_recv()
+
+    P = functools.partial
+    near_tasks = (begin, finish)
+    far_tasks = (far_begin, far_finish)
 
     @pl.when(outer)
     def _():
-        def which(n):
-            return 0, n % 2, n // 2
-
-        run(0, 6, which)
-        corner_landed()
-        finish(*which(5))
-        run(6, 8, which)
-        finish(*which(7))
+        run(8, [(lambda n: n >= 0, lambda n: (0, n % 2, n // 2), near_tasks)], {
+            0: [lambda: loop(0, steps, from_z)],
+            2: [lambda: loop(0, steps, from_y)],
+            6: [corner_landed],
+        })
 
     @pl.when(inner)
     def _():
-        loop(steps - lag, chunks, lambda k: side_on(1, k))
-        loop(0, first, relay_on)
-        loop(0, chunks, lambda k: w_landed(1, 1 - x, k))
-
-        def which(n):
-            return (n % 4) // 2, n % 2, n // 4
-
-        per = 12 // (chunks - first)
-
-        def mixed(k):
-            relay_on(k)
-            for m in range(per):
-                n = (k - first) * per + m
-                begin(*which(n))
-
-                @pl.when(n > 0)
-                def _():
-                    finish(*which(n - 1))
-
-            side_on(2, k - first)
-
-        loop(first, chunks, mixed)
-        run(per * (chunks - first), 12, which)
-        finish(*which(11))
-        loop(chunks - first, chunks - 1, lambda k: side_on(2, k))
-        corner_landed()
-        run(12, 16, which)
-        finish(*which(15))
-        side_on(2, chunks - 1)
-
-        def last(n):
-            return 2, jnp.where(n < 4, x, 1 - x), n % 4
-
-        run(0, 4, last)
-        loop(0, chunks, lambda k: w_landed(2, 1 - x, k))
-        finish(*last(3))
-        run(4, 8, last)
-        finish(*last(7))
-
-    def drain(t):
-        swap(t).wait_send()
-        s, u, slot = t // 8, (t // 4) % 2, t % 4
-
-        @pl.when(jnp.logical_not(stays(s, slot)))
-        def _():
-            out_copy(s, u, slot).wait_send()
-
-    loop(0, jnp.where(inner, 24, 8), drain)
-
-    def act_sent(i):
-        act_y(i).wait_send()
-        act_z(i).wait_send()
-
-        @pl.when(i >= over_z)
-        def _():
-            on_z(i).wait_send()
-
-        @pl.when(i < over_y)
-        def _():
-            on_y(i).wait_send()
-
-    loop(0, steps, act_sent)
-
-    def weight_sent(k):
-        @pl.when(outer)
-        def _():
-            to_relay(k).wait_send()
-
-        @pl.when(inner)
-        def _():
-            mid_own(k).wait_send()
-            mid_relay(k).wait_send()
-            side(1, k).wait_send()
-            side(2, k).wait_send()
-
-    loop(0, chunks, weight_sent)
-
-    def out_landed(n):
-        column = pl.ds(pl.multiple_of((n // 2) * unit, 128), unit)
-        ref = out_ref.at[pl.ds(pl.multiple_of((n % 2) * rows_mine, rows_mine), rows_mine), column]
-        remote(stage.at[0], ref, out_send.at[0], out_recv.at[n], (group, dp, other)).wait_recv()
-
-    loop(0, 16, out_landed)
+        def is_far(n):
+            return jnp.logical_or(n >= 18, jnp.logical_and(n >= 12, n < 14))
+
+        def near_which(n):
+            m = jnp.where(n < 12, n, n - 2)
+            return (m % 4) // 2, m % 2, m // 4
+
+        def far_which(n):
+            late = n >= 20
+            return (jnp.where(n < 14, n - 12, jnp.where(late, 2 + (n - 20) // 2, n - 18)),
+                    jnp.where(n < 14, 0, jnp.where(late, 1 - n % 2, 1)))
+
+        kinds = [(lambda n: jnp.logical_not(is_far(n)), near_which, near_tasks), (is_far, far_which, far_tasks)]
+        run(24, kinds, {
+            0: [P(side_on, 1, 3), P(relay_on, 1)],
+            1: [P(side_on, 1, 4), P(from_z, 0), P(from_z, 1), P(from_z, 2)],
+            2: [P(side_on, 1, 5), P(from_z, 3), P(side_on, 1, 6), P(relay_on, 2), P(side_on, 1, 7), P(from_z, 4),
+                lambda: loop(0, steps, from_y), P(side_on, 2, 0), P(from_z, 5),
+                near_swapped],
+            3: [P(relay_on, 3)],
+            4: [P(side_on, 2, 1)],
+            6: [P(from_z, 6), P(side_on, 2, 2)],
+            8: [P(from_z, 7), P(side_on, 2, 3)],
+            9: [P(relay_on, 4)],
+            11: [P(relay_on, 5)],
+            12: [P(side_on, 2, 4)],
+            13: [P(far_swapped, 0)],
+            14: [P(relay_on, 6), P(side_on, 2, 5), P(relay_on, 7), corner_landed, P(side_on, 2, 6)],
+            15: [P(side_on, 2, 7)],
+            22: [P(far_swapped, 1)],
+        })
+
+    def sent(ref, sem):
+        remote(ref, ref, sem, sem, (group, dp, other)).wait_send()
+
+    def sent_if(holds, ref, sem):
+        @pl.when(holds)
+        def _():
+            sent(ref, sem)
+
+    sent(act.at[0], act_send.at[0])
+    sent(act.at[0], act_send.at[1])
+    unit_ref = wall.at[0, 0]
+    sent(unit_ref, w_send.at[0])
+    far_goes = jnp.logical_and(inner, core == half)
+    far_mate = jnp.logical_and(inner, core != half)
+    sent_if(inner, stage.at[0:14], out_send.at[0])
+    sent_if(jnp.logical_and(outer, core == half), stage.at[0:6], out_send.at[0])
+    sent_if(jnp.logical_and(outer, core != half), stage.at[0:8], out_send.at[0])
+    sent_if(inner, px_out, px_send.at[0])
+    sent_if(outer, px_out.at[0:8], px_send.at[0])
+    sent_if(inner, far_out, px_send.at[1])
+    sent_if(far_goes, far_stage, out_send.at[1])
+    sent_if(far_mate, far_stage.at[0:3], out_send.at[1])
+    for n in range(1, 4):
+        sent_if(inner, unit_ref, w_send.at[n])
+
+    def columns(low, high):
+        return act.at[0, :, low * step_cols:high * step_cols]
+
+    for holds, y_count, z_count in ((inner, near, steps - far), (outer, far, steps - near)):
+        if y_count:
+            sent_if(holds, columns(0, y_count), act_send.at[2])
+        if z_count:
+            sent_if(holds, columns(0, z_count), act_send.at[3])
+
+    remote(out_ref, out_ref, out_recv.at[0], out_recv.at[0], (group, dp, other)).wait_recv()
 
 
 def square_program(line, queries, fresh_keys, fresh_values, key_pages, value_pages, table, lengths, weight):
@@ -771,7 +852,7 @@
     unit = cols // 2
     span = table.shape[1] * PAGE_TOKENS + tokens
     kv_width = fresh_keys.shape[1]
-    vmem = pl.BlockSpec(memory_space=pltpu.VMEM)
+    hbm = pl.BlockSpec(memory_space=pl.ANY)
     smem = pl.BlockSpec(memory_space=pltpu.SMEM)
     dma = pltpu.SemaphoreType.DMA
     bf16, f32 = jnp.bfloat16, jnp.float32
@@ -780,31 +861,39 @@
     return pl.pallas_call(
         functools.partial(square_kernel, line),
         out_shape=jax.ShapeDtypeStruct((tokens, line * cols), bf16),
-        in_specs=[vmem, vmem, vmem, vmem, vmem, smem, smem, pl.BlockSpec(memory_space=pl.ANY)],
-        out_specs=vmem,
+        in_specs=[hbm, hbm, hbm, hbm, hbm, smem, smem, hbm],
+        out_specs=hbm,
         scratch_shapes=[
+            pltpu.VMEM(queries.shape, bf16),
+            pltpu.VMEM(key_pages.shape, bf16),
+            pltpu.VMEM(value_pages.shape, bf16),
             pltpu.VMEM((4, tokens, wide), bf16),
             pltpu.VMEM((3, 2, part, unit), bf16),
             pltpu.VMEM((part, unit), bf16),
-            pltpu.VMEM((24, tokens // 2, unit), bf16),
-            pltpu.VMEM((24, tokens // 2, unit), bf16),
-            pltpu.VMEM((24, tokens, unit), f32),
-            pltpu.VMEM((24, tokens // 2, unit), bf16),
+            pltpu.VMEM((16, tokens // 2, unit), bf16),
+            pltpu.VMEM((16, tokens // 2, unit), bf16),
+            pltpu.VMEM((16, tokens, unit), f32),
+            pltpu.VMEM((16, tokens // 2, unit), bf16),
             pltpu.VMEM((span, kv_width), bf16),
             pltpu.VMEM((span, kv_width), bf16),
             pltpu.VMEM((tokens, span), f32),
-            dma((2, 2, chunks)),
             dma((2, chunks)),
-            dma((2, chunks)),
+            dma((3,)),
+            dma((4,)),
             dma((chunks,)),
             dma((2,)),
-            dma((3, steps)),
-            dma((2, steps)),
-            dma((2, steps)),
-            dma((24,)),
-            dma((24,)),
+            dma((2, steps + 1)),
+            dma((4,)),
             dma((16,)),
-            dma((24,)),
+            dma((2,)),
+            dma((1,)),
+            dma((2,)),
+            dma((5,)),
+            pltpu.VMEM((4, 4, tokens // 2, unit // 2), bf16),
+            pltpu.VMEM((4, 4, tokens // 2, unit // 2), bf16),
+            pltpu.VMEM((4, 4, tokens, unit // 2), f32),
+            pltpu.VMEM((4, 4, tokens // 2, unit // 2), bf16),
+            dma((4, 2)),
         ],
         compiler_params=pltpu.CompilerParams(
             collective_id=0, has_side_effects=True, vmem_limit_bytes=60 * 1024 * 1024

time: 92.1 us -> 74.3 us (0.81)
  Pallas kernels: 89.6 us -> 71.8 us
    pallas_call x1, Pallas kernels: 89.6 us -> 71.8 us  [square_program(): pl.pallas_call(functools.partial(square_kernel, line), out_shape=jax.Shap...]
where the time goes in v2:
time: 74.3 us; the launch traced here: 74.1 us
  Pallas kernels  71.8 us (97%)
  local copies, waits for them, and re-layouts  2.3 us (3%)
    pallas_call x1, Pallas kernels, square_program(): pl.pallas_call(functools.partial(square_kernel, line), out_shape=jax.Shap...  71.8 us
    unnamed x1, local copies, waits for them, and re-layouts  2.3 us

profile of v2, /device:TPU:1, one launch (start us, length us, event | category | flops | bytes accessed | tf_op | source)
XLA Modules:
  0.0 74.1 jit_solution(14470018569882122115)
XLA Ops:
  0.0 71.8 %shard_map.82 = bf16[256,2048]{1,0:T(8,128)(2,1)} custom-call(bf16[256,2048]{1,0:T(8,128)(2,1)} %q_hbm.1, bf16[256,256]{1,0:T(8,128)(2,1)} %fk_hbm.1, bf16[256,256]{1,0:T(8,128)(2,1)} %fv_hbm.1, bf16[10,128,256]{2,1,0:T(8,128)(2,1)} %kp_hbm.1, bf16[10,128,256]{2,1,0:T(8,128)(2,1)} %vp_hbm.1, s32[1,8]{1,0:T(1,128)} %table_ref.1, s32[8]{0:T(128)} %len_ref.1, ...), custom_call_target="tpu_custom_call" | custom-call | flops 9126805504 | bytes 8388608 | tf_op jit(solution)/shard_map/pallas_call | solution.py:861
  71.8 2.3 %copy.10 = bf16[256,2048]{1,0:T(8,128)(2,1)} copy(bf16[256,2048]{1,0:T(8,128)(2,1)} %shard_map.82) | data formatting | bytes 2097152

commit v3 on v2

--- a/solution.py
+++ b/solution.py
@@ -11,7 +11,7 @@
 QUERY_GROUP = 8
 PAGE_TOKENS = 128
 CHUNK = 256
-OUTER_ZY = 7
+OUTER_ZY = 8
 INNER_ZY = 5
 SCALE = HEAD_SIZE ** (-0.5) * 1.4426950408889634
 MASKED = -1e30
@@ -405,7 +405,7 @@
 
 def square_kernel(
     line, q_hbm, fk_hbm, fv_hbm, kp_hbm, vp_hbm, table_ref, len_ref, w_ref, out_ref,
-    q_ref, kp_ref, vp_ref, act, wall, relay, px_out, px_in, keep, stage, keys, values, bias,
+    q_ref, kp_ref, vp_ref, act, wall, far_wall, relay, px_out, px_in, keep, stage, keys, values, bias,
     w_recv, w_swap, w_send, r_recv, own_sem, act_recv, act_send,
     px_recv, px_send, out_recv, out_send, in_sem,
     far_out, far_in, far_keep, far_stage, far_recv,
@@ -475,45 +475,54 @@
     pl.semaphore_wait(barrier, 7 + jnp.where(inner, 2, 0))
 
     half_cols = pl.ds(pl.multiple_of(x * unit, 128), unit)
+    half_lane = pl.ds(pl.multiple_of(x * lane, 128), lane)
+    rest_cols = pl.ds(pl.multiple_of((1 - x) * unit, 128), unit)
+    rest_lane = pl.ds(pl.multiple_of((1 - x) * lane, 128), lane)
     deep = chunks // 2
+    pieces = deep + chunks
 
     def patch(k):
-        return (pl.ds(pl.multiple_of(k % deep * tall, tall), tall),
-                pl.ds(pl.multiple_of(k // deep * lane, 128), lane))
+        if isinstance(k, jax.Array) or k < deep:
+            return 0, pl.ds(pl.multiple_of(k * tall, tall), tall)
+        return 1, pl.ds((k - deep) * CHUNK, CHUNK)
 
     def mid_own(k):
         return remote(
-            w_ref.at[rows(k), half_cols], wall.at[1, x, rows(k)],
+            w_ref.at[rows(k), half_cols], wall.at[1, rows(k), half_cols],
             w_send.at[0], w_recv.at[0, k], (group, zm * 2 + y, core),
         )
 
     def to_relay(k):
+        v, part_rows = patch(k)
+        column = pl.ds(pl.multiple_of(x * unit + v * lane, 128), lane)
         return remote(
-            w_ref.at[patch(k)[0], pl.ds(pl.multiple_of(x * unit + k // deep * lane, 128), lane)], relay.at[patch(k)],
+            w_ref.at[part_rows, column], relay.at[v, part_rows],
             w_send.at[0], r_recv.at[k], (group, zp * 2 + y, core),
         )
 
     def mid_relay(k):
+        v, part_rows = patch(k)
         return remote(
-            relay.at[patch(k)], wall.at[2, x, *patch(k)],
+            relay.at[v, part_rows], far_wall.at[v, part_rows, half_lane],
             w_send.at[1], w_recv.at[1, k], (group, zm * 2 + y, core),
         )
 
     def side(s, k):
         if s == 1:
-            ref, sem = wall.at[s, x, rows(k)], w_swap.at[0]
+            ref, sem = wall.at[1, rows(k), half_cols], w_swap.at[0]
         else:
-            ref, sem = wall.at[s, x, *patch(k)], w_swap.at[1 + k // deep]
+            v, part_rows = patch(k)
+            ref, sem = far_wall.at[v, part_rows, half_lane], w_swap.at[1 + v]
         return remote(ref, ref, w_send.at[s + 1], sem, (cousin, dp, core))
 
     def swapped(ref, n):
         remote(ref, ref, w_send.at[2], w_swap.at[n], (cousin, dp, core)).wait_recv()
 
     def near_swapped():
-        swapped(wall.at[1, 1 - x], 0)
+        swapped(wall.at[1, :, rest_cols], 0)
 
     def far_swapped(v):
-        swapped(wall.at[2, 1 - x, :, v * lane:(v + 1) * lane], 1 + v)
+        swapped(far_wall.at[v, :, rest_lane], 1 + v)
 
     def relay_on(k):
         to_relay(k).wait_recv()
@@ -523,10 +532,8 @@
         (mid_own(k) if s == 1 else mid_relay(k)).wait_recv()
         side(s, k).start()
 
-    def own_copy(u):
-        return pltpu.make_async_copy(
-            w_ref.at[:, u * unit:(u + 1) * unit], wall.at[0, u], own_sem.at[u]
-        )
+    def own_copy():
+        return pltpu.make_async_copy(w_ref, wall.at[0], own_sem.at[0])
 
     @pl.when(inner)
     def _():
@@ -536,8 +543,7 @@
     def _():
         to_relay(0).start()
 
-    own_copy(0).start()
-    own_copy(1).start()
+    own_copy().start()
 
     length = len_ref[dp]
     position = lax.broadcasted_iota(jnp.int32, (tokens, cached), 1)
@@ -573,22 +579,27 @@
         return remote(act_at(1, i), act_at(3, i), act_send.at[3], act_recv.at[1, steps],
                       (group, zp * 2 + y, core))
 
-    over_y = jnp.where(inner, near, far)
-    over_z = jnp.where(inner, far, near)
+    over_y = steps - jnp.where(inner, near, far)
+    over_z = steps - jnp.where(inner, far, near)
 
     def from_y(i):
         act_y(i).wait_recv()
 
-        @pl.when(i >= over_z)
+        @pl.when(i < over_z)
         def _():
             on_z(i).start()
 
     def from_z(i):
         act_z(i).wait_recv()
 
-        @pl.when(i < over_y)
+        @pl.when(i >= over_y)
         def _():
             on_y(i).start()
+
+    P = functools.partial
+
+    def own_y(i):
+        act_y(i).start()
 
     def attention_step(i):
         kv = (i * heads_per_step) // QUERY_GROUP
@@ -606,135 +617,122 @@
                 weights.astype(jnp.bfloat16), values[:, kv_cols], preferred_element_type=jnp.float32
             )
             act[0, :, pl.ds(start, HEAD_SIZE)] = (weighted / total).astype(jnp.bfloat16)
-        act_y(i).start()
         act_z(i).start()
 
-        @pl.when(jnp.logical_and(outer, i % 2 == 1))
+        @pl.when(jnp.logical_or(outer, i < 2))
+        def _():
+            act_y(i).start()
+
+        @pl.when(jnp.logical_and(outer, jnp.logical_and(i % 2 == 1, i < 2 * deep - 2)))
         def _():
             to_relay((i + 1) // 2).start()
 
-        @pl.when(jnp.logical_and(inner, jnp.logical_and(i >= 3, i % 2 == 1)))
-        def _():
-            side_on(1, (i - 3) // 2)
-
-        @pl.when(jnp.logical_and(inner, i == 3))
-        def _():
-            relay_on(0)
+        def at(n, *todo):
+            @pl.when(jnp.logical_and(inner, i == n))
+            def _():
+                for act_now in todo:
+                    act_now()
+
+        at(3, P(side_on, 1, 0), P(relay_on, 0))
+        at(4, P(from_z, 0), P(own_y, 2))
+        at(5, P(side_on, 1, 1), P(from_y, 0))
+        at(7, P(side_on, 1, 2), P(from_z, 1), P(own_y, 3))
 
     loop(0, steps, attention_step)
 
     @pl.when(outer)
     def _():
-        loop(steps // 2 + 1, chunks, lambda k: to_relay(k).start())
+        for k in range(deep, pieces):
+            to_relay(k).start()
 
     def shard_z(s):
         return jnp.where(s == 0, z, zm)
 
-    def task(s, u, slot):
-        return (s * 2 + u) * 4 + slot
+    def task(s, slot):
+        return s * 4 + slot
 
     def swap(t):
         return remote(px_out.at[t], px_in.at[t], px_send.at[0], px_recv.at[t], (group, dp, other))
 
-    def place(s, u):
+    my_rows = pl.ds(pl.multiple_of(core * rows_mine, rows_mine), rows_mine)
+    mate_rows = pl.ds(pl.multiple_of(other * rows_mine, rows_mine), rows_mine)
+
+    def place(s):
         zs = shard_z(s)
         to = zs // 2
-        column = (zs * 2 + y - to * line) * cols + u * unit
-        ref = out_ref.at[pl.ds(pl.multiple_of(core * rows_mine, rows_mine), rows_mine),
-                         pl.ds(pl.multiple_of(column, 128), unit)]
-        return to, ref
-
-    def out_copy(s, u, slot):
-        to, ref = place(s, u)
-        t = task(s, u, slot)
-        zd = jnp.where(slot >= 2, zp, z)
-        yd = jnp.where(slot % 2 == 1, 1 - y, y)
-        return remote(stage.at[t], ref, out_send.at[0], out_recv.at[0], (group, zd * 2 + yd, to))
+        column = (zs * 2 + y - to * line) * cols
+        return to, out_ref.at[my_rows, pl.ds(pl.multiple_of(column, 128), cols)]
+
+    def owner(slot):
+        return jnp.where(slot >= 2, zp, z) * 2 + jnp.where(slot % 2 == 1, 1 - y, y)
 
     def stays(s, slot):
         return jnp.logical_and(slot == 0, shard_z(s) // 2 == core)
 
-    def begin(s, u, slot):
-        t = task(s, u, slot)
-        keep[t] = jnp.dot(act[slot], wall[s, u], preferred_element_type=jnp.float32)
-        start = pl.multiple_of(other * rows_mine, rows_mine)
-        px_out[t] = keep[t, pl.ds(start, rows_mine), :].astype(jnp.bfloat16)
+    def begin(s, slot):
+        t = task(s, slot)
+        keep[t] = jnp.dot(act[slot], wall[s], preferred_element_type=jnp.float32)
+        px_out[t] = keep[t, mate_rows, :].astype(jnp.bfloat16)
         swap(t).start()
 
-    def finish(s, u, slot):
-        t = task(s, u, slot)
+    def finish(s, slot):
+        t = task(s, slot)
         swap(t).wait_recv()
-        start = pl.multiple_of(core * rows_mine, rows_mine)
-        stage[t] = (keep[t, pl.ds(start, rows_mine), :] + px_in[t].astype(jnp.float32)).astype(jnp.bfloat16)
+        stage[t] = (keep[t, my_rows, :] + px_in[t].astype(jnp.float32)).astype(jnp.bfloat16)
+        to, ref = place(s)
 
         @pl.when(stays(s, slot))
         def _():
-            to, ref = place(s, u)
             pltpu.make_async_copy(stage.at[t], ref, out_recv.at[0]).start()
 
         @pl.when(jnp.logical_not(stays(s, slot)))
         def _():
-            out_copy(s, u, slot).start()
-
-    def strip(w):
-        return jnp.where(w % 2 == 0, x, 1 - x), w // 2
-
-    def far_swap(w, p):
+            remote(stage.at[t], ref, out_send.at[0], out_recv.at[0], (group, owner(slot), to)).start()
+
+    def far_swap(v, p):
         pair = pl.ds(p * 2, 2)
-        return remote(far_out.at[w, pair], far_in.at[w, pair], px_send.at[1], far_recv.at[w, p],
+        return remote(far_out.at[v, pair], far_in.at[v, pair], px_send.at[1], far_recv.at[v, p],
                       (group, dp, other))
 
-    def far_begin(w, p):
-        u, v = strip(w)
+    def far_begin(v, p):
         pair = pl.ds(p * 2, 2)
-        far_keep[w, pair] = jnp.dot(
-            act[pair].reshape(2 * tokens, wide), wall[2, u, :, pl.ds(pl.multiple_of(v * lane, 128), lane)],
-            preferred_element_type=jnp.float32,
-        ).reshape(2, tokens, lane)
-        start = pl.multiple_of(other * rows_mine, rows_mine)
-        far_out[w, pair] = far_keep[w, pair, pl.ds(start, rows_mine), :].astype(jnp.bfloat16)
-        far_swap(w, p).start()
-
-    def far_place(w):
-        u, v = strip(w)
+        far_keep[v, pair] = jnp.dot(
+            act[pair].reshape(2 * tokens, wide), far_wall[v], preferred_element_type=jnp.float32,
+        ).reshape(2, tokens, unit)
+        far_out[v, pair] = far_keep[v, pair, mate_rows, :].astype(jnp.bfloat16)
+        far_swap(v, p).start()
+
+    def far_stays(slot):
+        return jnp.logical_and(slot == 0, 1 - half == core)
+
+    def far_finish(v, p):
+        far_swap(v, p).wait_recv()
+        pair = pl.ds(p * 2, 2)
+        far_stage[v, pair] = (
+            far_keep[v, pair, my_rows, :] + far_in[v, pair].astype(jnp.float32)
+        ).astype(jnp.bfloat16)
         zs = (line - 1) * (1 - half)
         to = zs // 2
-        column = (zs * 2 + y - to * line) * cols + u * unit + v * lane
-        ref = out_ref.at[pl.ds(pl.multiple_of(core * rows_mine, rows_mine), rows_mine),
-                         pl.ds(pl.multiple_of(column, 128), lane)]
-        return to, ref
-
-    def far_copy(w, slot):
-        to, ref = far_place(w)
-        zd = jnp.where(slot >= 2, zp, z)
-        yd = jnp.where(slot % 2 == 1, 1 - y, y)
-        return remote(far_stage.at[w, slot], ref, out_send.at[1], out_recv.at[0], (group, zd * 2 + yd, to))
-
-    def far_stays(slot):
-        return jnp.logical_and(slot == 0, 1 - half == core)
-
-    def far_finish(w, p):
-        far_swap(w, p).wait_recv()
-        pair = pl.ds(p * 2, 2)
-        start = pl.multiple_of(core * rows_mine, rows_mine)
-        far_stage[w, pair] = (
-            far_keep[w, pair, pl.ds(start, rows_mine), :] + far_in[w, pair].astype(jnp.float32)
-        ).astype(jnp.bfloat16)
-        far_copy(w, p * 2 + 1).start()
-
-        @pl.when(far_stays(p * 2))
-        def _():
-            to, ref = far_place(w)
-            pltpu.make_async_copy(far_stage.at[w, p * 2], ref, out_recv.at[0]).start()
-
-        @pl.when(jnp.logical_not(far_stays(p * 2)))
-        def _():
-            far_copy(w, p * 2).start()
-
-    own_copy(0).wait()
-    own_copy(1).wait()
-
-    def run(count, kinds, duties):
+        for n in (1, 0):
+            slot = p * 2 + n
+            for u in range(2):
+                column = (zs * 2 + y - to * line) * cols + u * unit + v * lane
+                ref = out_ref.at[my_rows, pl.ds(pl.multiple_of(column, 128), lane)]
+                src = far_stage.at[v, slot, :, u * lane:(u + 1) * lane]
+                if n:
+                    remote(src, ref, out_send.at[1], out_recv.at[0], (group, owner(slot), to)).start()
+                else:
+                    @pl.when(far_stays(slot))
+                    def _():
+                        pltpu.make_async_copy(src, ref, out_recv.at[0]).start()
+
+                    @pl.when(jnp.logical_not(far_stays(slot)))
+                    def _():
+                        remote(src, ref, out_send.at[1], out_recv.at[0], (group, owner(slot), to)).start()
+
+    own_copy().wait()
+
+    def run(count, kinds, duties, prompt):
         def each(n, what):
             for holds, which, acts in kinds:
                 @pl.when(holds(n))
@@ -742,6 +740,8 @@
                     acts[what](*which(n))
 
         def one(n):
+            early = functools.reduce(jnp.logical_or, [n == m + 1 for m in prompt])
+
             for at, todo in duties.items():
                 @pl.when(n == at)
                 def _():
@@ -752,7 +752,7 @@
             def _():
                 each(n, 0)
 
-            @pl.when(n > 0)
+            @pl.when(jnp.logical_and(n > 0, jnp.logical_not(early)))
             def _():
                 each(n - 1, 1)
 
@@ -761,51 +761,46 @@
     def corner_landed():
         remote(act.at[2], act.at[3], act_send.at[2], act_recv.at[1, steps], (group, peer, core)).wait_recv()
 
-    P = functools.partial
     near_tasks = (begin, finish)
     far_tasks = (far_begin, far_finish)
 
     @pl.when(outer)
     def _():
-        run(8, [(lambda n: n >= 0, lambda n: (0, n % 2, n // 2), near_tasks)], {
-            0: [lambda: loop(0, steps, from_z)],
-            2: [lambda: loop(0, steps, from_y)],
-            6: [corner_landed],
-        })
+        run(4, [(lambda n: n >= 0, lambda n: (0, n), near_tasks)], {
+            1: [P(finish, 0, 0), lambda: loop(0, steps, from_z), lambda: loop(0, steps, from_y)],
+            3: [P(finish, 0, 2), corner_landed],
+        }, (0, 2))
 
     @pl.when(inner)
     def _():
         def is_far(n):
-            return jnp.logical_or(n >= 18, jnp.logical_and(n >= 12, n < 14))
+            return jnp.logical_or(n >= 9, n == 6)
 
         def near_which(n):
-            m = jnp.where(n < 12, n, n - 2)
-            return (m % 4) // 2, m % 2, m // 4
+            m = jnp.where(n < 7, n, n - 1)
+            group = m // 2
+            return m % 2, jnp.where(group == 0, 0, jnp.where(group == 3, 1, group + 1))
 
         def far_which(n):
-            late = n >= 20
-            return (jnp.where(n < 14, n - 12, jnp.where(late, 2 + (n - 20) // 2, n - 18)),
-                    jnp.where(n < 14, 0, jnp.where(late, 1 - n % 2, 1)))
+            return n // 10, jnp.where(n % 4 == 2, 1, 0)
 
         kinds = [(lambda n: jnp.logical_not(is_far(n)), near_which, near_tasks), (is_far, far_which, far_tasks)]
-        run(24, kinds, {
-            0: [P(side_on, 1, 3), P(relay_on, 1)],
-            1: [P(side_on, 1, 4), P(from_z, 0), P(from_z, 1), P(from_z, 2)],
-            2: [P(side_on, 1, 5), P(from_z, 3), P(side_on, 1, 6), P(relay_on, 2), P(side_on, 1, 7), P(from_z, 4),
-                lambda: loop(0, steps, from_y), P(side_on, 2, 0), P(from_z, 5),
-                near_swapped],
-            3: [P(relay_on, 3)],
-            4: [P(side_on, 2, 1)],
-            6: [P(from_z, 6), P(side_on, 2, 2)],
-            8: [P(from_z, 7), P(side_on, 2, 3)],
-            9: [P(relay_on, 4)],
-            11: [P(relay_on, 5)],
-            12: [P(side_on, 2, 4)],
-            13: [P(far_swapped, 0)],
-            14: [P(relay_on, 6), P(side_on, 2, 5), P(relay_on, 7), corner_landed, P(side_on, 2, 6)],
-            15: [P(side_on, 2, 7)],
-            22: [P(far_swapped, 1)],
-        })
+        run(12, kinds, {
+            0: [P(side_on, 1, 3), P(relay_on, 1), P(from_y, 1)],
+            1: [P(side_on, 1, 4), P(from_z, 2), P(from_y, 2), P(finish, 0, 0), P(side_on, 1, 5), P(from_z, 3), P(own_y, 4),
+                P(side_on, 1, 6), P(relay_on, 2), P(side_on, 1, 7), P(from_z, 4), P(from_z, 5), P(own_y, 5),
+                P(side_on, 2, 0), P(relay_on, 3), P(side_on, 2, 1), near_swapped],
+            2: [P(from_z, 6), P(side_on, 2, 2), P(from_z, 7), P(own_y, 6), P(own_y, 7)],
+            3: [P(relay_on, 4), P(side_on, 2, 3)],
+            4: [P(relay_on, 5), P(relay_on, 6), P(finish, 1, 2), P(side_on, 2, 4), P(relay_on, 7), P(side_on, 2, 5),
+                P(relay_on, 8), corner_landed],
+            5: [P(side_on, 2, 6), P(relay_on, 9)],
+            6: [P(side_on, 2, 7), P(relay_on, 10), P(far_swapped, 0)],
+            7: [P(side_on, 2, 8), P(relay_on, 11), lambda: loop(3, steps, from_y)],
+            8: [P(side_on, 2, 9), P(side_on, 2, 10)],
+            9: [P(side_on, 2, 11)],
+            10: [P(far_finish, 0, 0), P(far_swapped, 1)],
+        }, (0, 3, 9))
 
     def sent(ref, sem):
         remote(ref, ref, sem, sem, (group, dp, other)).wait_send()
@@ -817,18 +812,18 @@
 
     sent(act.at[0], act_send.at[0])
     sent(act.at[0], act_send.at[1])
-    unit_ref = wall.at[0, 0]
+    unit_ref = wall.at[0, :, 0:unit]
     sent(unit_ref, w_send.at[0])
     far_goes = jnp.logical_and(inner, core == half)
     far_mate = jnp.logical_and(inner, core != half)
-    sent_if(inner, stage.at[0:14], out_send.at[0])
-    sent_if(jnp.logical_and(outer, core == half), stage.at[0:6], out_send.at[0])
-    sent_if(jnp.logical_and(outer, core != half), stage.at[0:8], out_send.at[0])
+    sent_if(inner, stage.at[0:7], out_send.at[0])
+    sent_if(jnp.logical_and(outer, core == half), stage.at[0:3], out_send.at[0])
+    sent_if(jnp.logical_and(outer, core != half), stage.at[0:4], out_send.at[0])
     sent_if(inner, px_out, px_send.at[0])
-    sent_if(outer, px_out.at[0:8], px_send.at[0])
+    sent_if(outer, px_out.at[0:4], px_send.at[0])
     sent_if(inner, far_out, px_send.at[1])
     sent_if(far_goes, far_stage, out_send.at[1])
-    sent_if(far_mate, far_stage.at[0:3], out_send.at[1])
+    sent_if(far_mate, far_stage.at[:, 0:3], out_send.at[1])
     for n in range(1, 4):
         sent_if(inner, unit_ref, w_send.at[n])
 
@@ -868,32 +863,33 @@
             pltpu.VMEM(key_pages.shape, bf16),
             pltpu.VMEM(value_pages.shape, bf16),
             pltpu.VMEM((4, tokens, wide), bf16),
-            pltpu.VMEM((3, 2, part, unit), bf16),
-            pltpu.VMEM((part, unit), bf16),
-            pltpu.VMEM((16, tokens // 2, unit), bf16),
-            pltpu.VMEM((16, tokens // 2, unit), bf16),
-            pltpu.VMEM((16, tokens, unit), f32),
-            pltpu.VMEM((16, tokens // 2, unit), bf16),
+            pltpu.VMEM((2, part, cols), bf16),
+            pltpu.VMEM((2, part, unit), bf16),
+            pltpu.VMEM((2, part, unit // 2), bf16),
+            pltpu.VMEM((8, tokens // 2, cols), bf16),
+            pltpu.VMEM((8, tokens // 2, cols), bf16),
+            pltpu.VMEM((8, tokens, cols), f32),
+            pltpu.VMEM((8, tokens // 2, cols), bf16),
             pltpu.VMEM((span, kv_width), bf16),
             pltpu.VMEM((span, kv_width), bf16),
             pltpu.VMEM((tokens, span), f32),
-            dma((2, chunks)),
+            dma((2, chunks + chunks // 2)),
             dma((3,)),
             dma((4,)),
-            dma((chunks,)),
-            dma((2,)),
+            dma((chunks + chunks // 2,)),
+            dma((1,)),
             dma((2, steps + 1)),
             dma((4,)),
-            dma((16,)),
+            dma((8,)),
             dma((2,)),
             dma((1,)),
             dma((2,)),
             dma((5,)),
-            pltpu.VMEM((4, 4, tokens // 2, unit // 2), bf16),
-            pltpu.VMEM((4, 4, tokens // 2, unit // 2), bf16),
-            pltpu.VMEM((4, 4, tokens, unit // 2), f32),
-            pltpu.VMEM((4, 4, tokens // 2, unit // 2), bf16),
-            dma((4, 2)),
+            pltpu.VMEM((2, 4, tokens // 2, unit), bf16),
+            pltpu.VMEM((2, 4, tokens // 2, unit), bf16),
+            pltpu.VMEM((2, 4, tokens, unit), f32),
+            pltpu.VMEM((2, 4, tokens // 2, unit), bf16),
+            dma((2, 2)),
         ],
         compiler_params=pltpu.CompilerParams(
             collective_id=0, has_side_effects=True, vmem_limit_bytes=60 * 1024 * 1024

time: 74.3 us -> 70.3 us (0.946)
  Pallas kernels: 71.8 us -> 67.8 us
    pallas_call x1, Pallas kernels: 71.8 us -> 67.8 us  [square_program(): pl.pallas_call(functools.partial(square_kernel, line), out_shape=jax.Shap...]
where the time goes in v3:
time: 70.3 us; the launch traced here: 70.1 us
  Pallas kernels  67.8 us (96%)
  local copies, waits for them, and re-layouts  2.3 us (3%)
    pallas_call x1, Pallas kernels, square_program(): pl.pallas_call(functools.partial(square_kernel, line), out_shape=jax.Shap...  67.8 us
    unnamed x1, local copies, waits for them, and re-layouts  2.3 us

profile of v3, /device:TPU:1, one launch (start us, length us, event | category | flops | bytes accessed | tf_op | source)
XLA Modules:
  0.0 70.1 jit_solution(18319942251734775585)
XLA Ops:
  0.0 67.8 %shard_map.82 = bf16[256,2048]{1,0:T(8,128)(2,1)} custom-call(bf16[256,2048]{1,0:T(8,128)(2,1)} %q_hbm.1, bf16[256,256]{1,0:T(8,128)(2,1)} %fk_hbm.1, bf16[256,256]{1,0:T(8,128)(2,1)} %fv_hbm.1, bf16[10,128,256]{2,1,0:T(8,128)(2,1)} %kp_hbm.1, bf16[10,128,256]{2,1,0:T(8,128)(2,1)} %vp_hbm.1, s32[1,8]{1,0:T(1,128)} %table_ref.1, s32[8]{0:T(128)} %len_ref.1, ...), custom_call_target="tpu_custom_call" | custom-call | flops 9126805504 | bytes 8388608 | tf_op jit(solution)/shard_map/pallas_call | solution.py:856
  67.8 2.3 %copy.10 = bf16[256,2048]{1,0:T(8,128)(2,1)} copy(bf16[256,2048]{1,0:T(8,128)(2,1)} %shard_map.82) | data formatting | bytes 2097152

commit v4 on v3

--- a/solution.py
+++ b/solution.py
@@ -463,7 +463,7 @@
         pl.semaphore_signal(barrier, inc=1, device_id=where, device_id_type=pl.DeviceIdType.MESH)
 
     greet((group, dp, other))
-    for chip in (peer, zp * 2 + y, zp * 2 + 1 - y):
+    for chip in (peer, zp * 2 + y):
         greet((group, chip, core))
         greet((group, chip, other))
 
@@ -472,7 +472,7 @@
         greet((cousin, dp, core))
         greet((group, zm * 2 + y, core))
 
-    pl.semaphore_wait(barrier, 7 + jnp.where(inner, 2, 0))
+    pl.semaphore_wait(barrier, 5 + jnp.where(inner, 2, 0))
 
     half_cols = pl.ds(pl.multiple_of(x * unit, 128), unit)
     half_lane = pl.ds(pl.multiple_of(x * lane, 128), lane)
@@ -505,6 +505,13 @@
         return remote(
             relay.at[v, part_rows], far_wall.at[v, part_rows, half_lane],
             w_send.at[1], w_recv.at[1, k], (group, zm * 2 + y, core),
+        )
+
+    def slant(k):
+        v, part_rows = patch(k)
+        return remote(
+            relay.at[v, part_rows], far_wall.at[v, part_rows, half_lane],
+            w_send.at[3], w_swap.at[1 + v], (cousin, zm * 2 + y, core),
         )
 
     def side(s, k):
@@ -784,6 +791,7 @@
         def far_which(n):
             return n // 10, jnp.where(n % 4 == 2, 1, 0)
 
+        last = pieces - 1
         kinds = [(lambda n: jnp.logical_not(is_far(n)), near_which, near_tasks), (is_far, far_which, far_tasks)]
         run(12, kinds, {
             0: [P(side_on, 1, 3), P(relay_on, 1), P(from_y, 1)],
@@ -796,10 +804,9 @@
                 P(relay_on, 8), corner_landed],
             5: [P(side_on, 2, 6), P(relay_on, 9)],
             6: [P(side_on, 2, 7), P(relay_on, 10), P(far_swapped, 0)],
-            7: [P(side_on, 2, 8), P(relay_on, 11), lambda: loop(3, steps, from_y)],
-            8: [P(side_on, 2, 9), P(side_on, 2, 10)],
-            9: [P(side_on, 2, 11)],
-            10: [P(far_finish, 0, 0), P(far_swapped, 1)],
+            7: [P(side_on, 2, 8), P(relay_on, last), slant(last).start, P(side_on, 2, 9), lambda: loop(3, steps, from_y),
+                P(side_on, 2, 10)],
+            10: [P(far_finish, 0, 0), mid_relay(last).wait_recv, P(far_swapped, 1)],
         }, (0, 3, 9))
 
     def sent(ref, sem):

time: 70.3 us -> 70.3 us (level)
  no operation moved by 1% of the time
where the time goes in v4:
time: 70.3 us; the launch traced here: 70.1 us
  Pallas kernels  67.8 us (96%)
  local copies, waits for them, and re-layouts  2.3 us (3%)
    pallas_call x1, Pallas kernels, square_program(): pl.pallas_call(functools.partial(square_kernel, line), out_shape=jax.Shap...  67.8 us
    unnamed x1, local copies, waits for them, and re-layouts  2.3 us

profile of v4, /device:TPU:1, one launch (start us, length us, event | category | flops | bytes accessed | tf_op | source)
XLA Modules:
  0.0 70.1 jit_solution(4697127475713991466)
XLA Ops:
  0.0 67.8 %shard_map.82 = bf16[256,2048]{1,0:T(8,128)(2,1)} custom-call(bf16[256,2048]{1,0:T(8,128)(2,1)} %q_hbm.1, bf16[256,256]{1,0:T(8,128)(2,1)} %fk_hbm.1, bf16[256,256]{1,0:T(8,128)(2,1)} %fv_hbm.1, bf16[10,128,256]{2,1,0:T(8,128)(2,1)} %kp_hbm.1, bf16[10,128,256]{2,1,0:T(8,128)(2,1)} %vp_hbm.1, s32[1,8]{1,0:T(1,128)} %table_ref.1, s32[8]{0:T(128)} %len_ref.1, ...), custom_call_target="tpu_custom_call" | custom-call | flops 9126805504 | bytes 8388608 | tf_op jit(solution)/shard_map/pallas_call | solution.py:863
  67.8 2.3 %copy.10 = bf16[256,2048]{1,0:T(8,128)(2,1)} copy(bf16[256,2048]{1,0:T(8,128)(2,1)} %shard_map.82) | data formatting | bytes 2097152

commit v5 on v4

--- a/solution.py
+++ b/solution.py
@@ -696,6 +696,30 @@
         def _():
             remote(stage.at[t], ref, out_send.at[0], out_recv.at[0], (group, owner(slot), to)).start()
 
+    def half_swap(p, h):
+        pair = pl.ds(p * 2, 2)
+        column = pl.ds(pl.multiple_of(h * lane, 128), lane)
+        return remote(far_out.at[1, pair, :, column], far_in.at[1, pair, :, column], px_send.at[1],
+                      far_recv.at[1 + h, p], (group, dp, other))
+
+    def half_begin(p, h):
+        pair = pl.ds(p * 2, 2)
+        column = pl.ds(pl.multiple_of(h * lane, 128), lane)
+        far_keep[1, pair, :, column] = jnp.dot(
+            act[pair].reshape(2 * tokens, wide), far_wall[1, :, column], preferred_element_type=jnp.float32,
+        ).reshape(2, tokens, lane)
+        far_out[1, pair, :, column] = far_keep[1, pair, mate_rows, column].astype(jnp.bfloat16)
+        half_swap(p, h).start()
+
+    def half_finish(p, h):
+        half_swap(p, h).wait_recv()
+        pair = pl.ds(p * 2, 2)
+        column = pl.ds(pl.multiple_of(h * lane, 128), lane)
+        far_stage[1, pair, :, column] = (
+            far_keep[1, pair, my_rows, column] + far_in[1, pair, :, column].astype(jnp.float32)
+        ).astype(jnp.bfloat16)
+        far_send(1, p, h)
+
     def far_swap(v, p):
         pair = pl.ds(p * 2, 2)
         return remote(far_out.at[v, pair], far_in.at[v, pair], px_send.at[1], far_recv.at[v, p],
@@ -718,24 +742,30 @@
         far_stage[v, pair] = (
             far_keep[v, pair, my_rows, :] + far_in[v, pair].astype(jnp.float32)
         ).astype(jnp.bfloat16)
+        far_send(v, p, 0)
+        far_send(v, p, 1)
+
+    def far_send(v, p, h):
         zs = (line - 1) * (1 - half)
         to = zs // 2
-        for n in (1, 0):
-            slot = p * 2 + n
-            for u in range(2):
-                column = (zs * 2 + y - to * line) * cols + u * unit + v * lane
-                ref = out_ref.at[my_rows, pl.ds(pl.multiple_of(column, 128), lane)]
-                src = far_stage.at[v, slot, :, u * lane:(u + 1) * lane]
-                if n:
-                    remote(src, ref, out_send.at[1], out_recv.at[0], (group, owner(slot), to)).start()
-                else:
-                    @pl.when(far_stays(slot))
-                    def _():
-                        pltpu.make_async_copy(src, ref, out_recv.at[0]).start()
-
-                    @pl.when(jnp.logical_not(far_stays(slot)))
-                    def _():
-                        remote(src, ref, out_send.at[1], out_recv.at[0], (group, owner(slot), to)).start()
+        column = (zs * 2 + y - to * line) * cols + h * unit + v * lane
+        ref = out_ref.at[my_rows, pl.ds(pl.multiple_of(column, 128), lane)]
+
+        def tile(slot):
+            return far_stage.at[v, slot, :, pl.ds(pl.multiple_of(h * lane, 128), lane)]
+
+        def go(slot):
+            remote(tile(slot), ref, out_send.at[1], out_recv.at[0], (group, owner(slot), to)).start()
+
+        go(p * 2 + 1)
+
+        @pl.when(far_stays(p * 2))
+        def _():
+            pltpu.make_async_copy(tile(p * 2), ref, out_recv.at[0]).start()
+
+        @pl.when(jnp.logical_not(far_stays(p * 2)))
+        def _():
+            go(p * 2)
 
     own_copy().wait()
 
@@ -770,6 +800,7 @@
 
     near_tasks = (begin, finish)
     far_tasks = (far_begin, far_finish)
+    half_tasks = (half_begin, half_finish)
 
     @pl.when(outer)
     def _():
@@ -781,7 +812,10 @@
     @pl.when(inner)
     def _():
         def is_far(n):
-            return jnp.logical_or(n >= 9, n == 6)
+            return jnp.logical_or(n == 9, n == 6)
+
+        def is_half(n):
+            return n >= 10
 
         def near_which(n):
             m = jnp.where(n < 7, n, n - 1)
@@ -789,11 +823,17 @@
             return m % 2, jnp.where(group == 0, 0, jnp.where(group == 3, 1, group + 1))
 
         def far_which(n):
-            return n // 10, jnp.where(n % 4 == 2, 1, 0)
+            return 0, jnp.where(n == 6, 1, 0)
+
+        def half_which(n):
+            return 1 - n % 2, jnp.where(n < 12, x, 1 - x)
 
         last = pieces - 1
-        kinds = [(lambda n: jnp.logical_not(is_far(n)), near_which, near_tasks), (is_far, far_which, far_tasks)]
-        run(12, kinds, {
+        kinds = [
+            (lambda n: jnp.logical_not(jnp.logical_or(is_far(n), is_half(n))), near_which, near_tasks),
+            (is_far, far_which, far_tasks), (is_half, half_which, half_tasks),
+        ]
+        run(14, kinds, {
             0: [P(side_on, 1, 3), P(relay_on, 1), P(from_y, 1)],
             1: [P(side_on, 1, 4), P(from_z, 2), P(from_y, 2), P(finish, 0, 0), P(side_on, 1, 5), P(from_z, 3), P(own_y, 4),
                 P(side_on, 1, 6), P(relay_on, 2), P(side_on, 1, 7), P(from_z, 4), P(from_z, 5), P(own_y, 5),
@@ -804,10 +844,11 @@
                 P(relay_on, 8), corner_landed],
             5: [P(side_on, 2, 6), P(relay_on, 9)],
             6: [P(side_on, 2, 7), P(relay_on, 10), P(far_swapped, 0)],
-            7: [P(side_on, 2, 8), P(relay_on, last), slant(last).start, P(side_on, 2, 9), lambda: loop(3, steps, from_y),
-                P(side_on, 2, 10)],
-            10: [P(far_finish, 0, 0), mid_relay(last).wait_recv, P(far_swapped, 1)],
-        }, (0, 3, 9))
+            7: [P(side_on, 2, 8), P(relay_on, last), slant(last).start, P(side_on, 2, 9), lambda: loop(3, steps, from_y)],
+            9: [P(side_on, 2, 10)],
+            10: [mid_relay(last).wait_recv],
+            12: [P(half_finish, 0, x), P(far_swapped, 1)],
+        }, (0, 3, 11))
 
     def sent(ref, sem):
         remote(ref, ref, sem, sem, (group, dp, other)).wait_send()
@@ -896,7 +937,7 @@
             pltpu.VMEM((2, 4, tokens // 2, unit), bf16),
             pltpu.VMEM((2, 4, tokens, unit), f32),
             pltpu.VMEM((2, 4, tokens // 2, unit), bf16),
-            dma((2, 2)),
+            dma((3, 2)),
         ],
         compiler_params=pltpu.CompilerParams(
             collective_id=0, has_side_effects=True, vmem_limit_bytes=60 * 1024 * 1024

time: 70.3 us -> 68.8 us (0.979)
  Pallas kernels: 67.8 us -> 66.3 us
    pallas_call x1, Pallas kernels: 67.8 us -> 66.3 us  [square_program(): pl.pallas_call(functools.partial(square_kernel, line), out_shape=jax.Shap...]
where the time goes in v5:
time: 68.8 us; the launch traced here: 68.6 us
  Pallas kernels  66.3 us (96%)
  local copies, waits for them, and re-layouts  2.3 us (3%)
    pallas_call x1, Pallas kernels, square_program(): pl.pallas_call(functools.partial(square_kernel, line), out_shape=jax.Shap...  66.3 us
    unnamed x1, local copies, waits for them, and re-layouts  2.3 us

profile of v5, /device:TPU:1, one launch (start us, length us, event | category | flops | bytes accessed | tf_op | source)
XLA Modules:
  0.0 68.6 jit_solution(8033417336027924910)
XLA Ops:
  0.0 66.3 %shard_map.82 = bf16[256,2048]{1,0:T(8,128)(2,1)} custom-call(bf16[256,2048]{1,0:T(8,128)(2,1)} %q_hbm.1, bf16[256,256]{1,0:T(8,128)(2,1)} %fk_hbm.1, bf16[256,256]{1,0:T(8,128)(2,1)} %fv_hbm.1, bf16[10,128,256]{2,1,0:T(8,128)(2,1)} %kp_hbm.1, bf16[10,128,256]{2,1,0:T(8,128)(2,1)} %vp_hbm.1, s32[1,8]{1,0:T(1,128)} %table_ref.1, s32[8]{0:T(128)} %len_ref.1, ...), custom_call_target="tpu_custom_call" | custom-call | flops 9126805504 | bytes 8388608 | tf_op jit(solution)/shard_map/pallas_call | solution.py:904
  66.3 2.3 %copy.10 = bf16[256,2048]{1,0:T(8,128)(2,1)} copy(bf16[256,2048]{1,0:T(8,128)(2,1)} %shard_map.82) | data formatting | bytes 2097152
